TPU v7x, 32 devices: a whole 2x2x4 slice. The times are simulated.
32 devices in a mesh: chain: 8 (over z, core), bond: 4 (over y, x).
Axes of the slice: x: 2, y: 2, z: 4, core: 2. Of those that a mesh axis runs over, the one named last changes fastest.
Arguments:
- sites: bfloat16 [8, 1024, 2048], P('chain', 'bond'), may hold values from -0.1875 to 0.1875
- start: bfloat16 [8, 1024, 1024], P('chain', 'bond'), may hold values from -0.125 to 0.125
- gates: float32 [8, 16], replicated, may hold values from -3 to 3
- bonds: int32 [9], replicated, may hold values from 512 to 1024, as said below
Outputs:
- new_sites: float32 [8, 1024, 2048], P('chain', 'bond')
Inputs may be any that keep to these rules, and one draw needn't show every extreme that they name: bonds[k] is the bond dimension of the cut just left of site k.
All inputs are finite; a program needn't handle non-finite values.
Results may differ from a plain program's by a relative error of at most 0.03.
Values may be sent and summed in bfloat16 or wider, within the bound.
A program may use at most 128 MiB of HBM per device.

v0:
```python
import jax
import jax.numpy as jnp
from jax import lax
from jax.experimental import pallas as pl
from jax.experimental.pallas import tpu as pltpu
from jax.sharding import PartitionSpec as P

ridge_ratio = 0.05
BLOCK = 128
SUB = 8


def partner(value, axis, apart):
    return lax.ppermute(value, axis, [(i, i ^ 1 << apart) for i in range(lax.axis_size(axis))])


def halves(x):
    high = x.astype(jnp.bfloat16)
    return high, (x - high.astype(jnp.float32)).astype(jnp.bfloat16)


def diagonal_inverse(tile):
    lane = lax.broadcasted_iota(jnp.int32, (SUB, BLOCK), 1)
    sub = lax.broadcasted_iota(jnp.int32, (SUB, BLOCK), 0)
    count = BLOCK // SUB
    rows = [tile[i * SUB : (i + 1) * SUB, :] for i in range(count)]
    full = (SUB, BLOCK)
    for b in range(count):
        base = b * SUB
        cols = [jnp.broadcast_to(rows[b][:, base + j : base + j + 1], full) for j in range(SUB)]
        current = rows[b]
        scale = jnp.zeros(full, jnp.float32)
        inverses, uppers, finals = [], {}, []
        for j in range(SUB):
            pivot = jnp.broadcast_to(cols[j][j : j + 1, :], full)
            inv = 1.0 / pivot
            inverses.append(inv)
            scale = jnp.where(sub == j, pivot, scale)
            m = jnp.where(sub > j, cols[j] * inv, 0.0)
            for k in range(j + 1, SUB):
                uppers[j, k] = jnp.broadcast_to(cols[k][j : j + 1, :], full)
                cols[k] = cols[k] - m * uppers[j, k]
            row = jnp.broadcast_to(current[j : j + 1, :], full)
            row = jnp.where(lane == base + j, 1.0, row)
            finals.append(jnp.where((lane > base + j) & (lane < base + SUB), 0.0, row))
            current = jnp.where((lane == base + j) & (sub >= j), jnp.where(sub == j, 1.0, 0.0), current) - m * row
        inside = (lane >= base) & (lane < base + SUB)
        for i in range(b + 1, count):
            held = [jnp.broadcast_to(rows[i][:, base + j : base + j + 1], full) for j in range(SUB)]
            fresh = jnp.where(inside, 0.0, rows[i])
            for j in range(SUB):
                c = held[j] * inverses[j]
                for k in range(j + 1, SUB):
                    held[k] = held[k] - c * uppers[j, k]
                fresh = fresh - c * finals[j]
            rows[i] = fresh
        rows[b] = jnp.where(lane <= base + sub, current * lax.rsqrt(scale), 0.0)
    return jnp.concatenate(rows, axis=0)


def turned(x):
    return x.astype(jnp.float32).T.astype(x.dtype)


def factor_kernel(bounds_ref, rows_ref, out_ref, right_ref):
    size = out_ref.shape[0]
    count = size // BLOCK
    wide = 2 * BLOCK
    for i in range(size // wide):
        left = turned(rows_ref[:, i * wide : (i + 1) * wide])
        out_ref[i * wide : (i + 1) * wide, i * wide :] = jnp.dot(
            left, rows_ref[:, i * wide :], preferred_element_type=jnp.float32
        )
    across = lax.broadcasted_iota(jnp.int32, (BLOCK, BLOCK), 1)
    eye = lax.broadcasted_iota(jnp.int32, (BLOCK, BLOCK), 0) == across
    kept = bounds_ref[1]
    diagonal = jnp.zeros((BLOCK, BLOCK), jnp.float32)
    for i in range(count):
        here = slice(i * BLOCK, (i + 1) * BLOCK)
        diagonal = diagonal + jnp.where(eye, out_ref[here, here], 0.0)
    trace = jnp.sum(jnp.sum(diagonal, axis=0, keepdims=True), axis=1, keepdims=True)
    ridge = ridge_ratio * trace / jnp.full((1, 1), kept, jnp.int32).astype(jnp.float32)
    for i in range(count):
        here = slice(i * BLOCK, (i + 1) * BLOCK)
        added = jnp.where(across + i * BLOCK < kept, jnp.broadcast_to(ridge, eye.shape), 1.0)
        out_ref[here, here] = out_ref[here, here] + jnp.where(eye, added, 0.0)

    def panel(k, carry):
        here = pl.ds(pl.multiple_of(k * BLOCK, BLOCK), BLOCK)
        inverse = diagonal_inverse(out_ref[here, here])
        inv_high, inv_low = halves(inverse)
        row_high, row_low = halves(out_ref[here, :])
        out_ref[here, :] = jnp.dot(
            jnp.concatenate([inv_high, inv_high, inv_low], axis=1),
            jnp.concatenate([row_high, row_low, row_high], axis=0),
            preferred_element_type=jnp.float32,
        )
        out_ref[here, here] = inverse
        high, low = halves(out_ref[here, :])
        right_ref[0:BLOCK, :] = high
        right_ref[BLOCK : 2 * BLOCK, :] = low
        right_ref[2 * BLOCK : 3 * BLOCK, :] = high

        def trailing(first, height):
            there = pl.ds(pl.multiple_of(first * BLOCK, BLOCK), height)
            left_high, left_low = halves(out_ref[here, there].T)
            out_ref[there, here] = jnp.zeros((height, BLOCK), jnp.float32)
            out_ref[there, :] = out_ref[there, :] - jnp.dot(
                jnp.concatenate([left_high, left_high, left_low], axis=1),
                right_ref[...],
                preferred_element_type=jnp.float32,
            )

        odd = (count - 1 - k) % 2

        @pl.when(odd == 1)
        def _():
            trailing(k + 1, BLOCK)

        def pair(i, inner):
            trailing(k + 1 + odd + 2 * i, wide)
            return inner

        lax.fori_loop(0, (count - 1 - k) // 2, pair, 0)
        column = lax.broadcasted_iota(jnp.int32, (BLOCK, size), 1)
        out_ref[here, :] = jnp.where(column < (k + 1) * BLOCK, out_ref[here, :], 0.0)
        return carry

    lax.fori_loop(0, count, panel, 0)


def factor_inverse(bounds, rows):
    size = rows.shape[1]
    return pl.pallas_call(
        factor_kernel,
        out_shape=jax.ShapeDtypeStruct((size, size), jnp.float32),
        in_specs=[pl.BlockSpec(memory_space=pltpu.SMEM), pl.BlockSpec(memory_space=pltpu.VMEM)],
        out_specs=pl.BlockSpec(memory_space=pltpu.VMEM),
        scratch_shapes=[pltpu.VMEM((3 * BLOCK, size), jnp.bfloat16)],
    )(bounds, rows)


CHUNK = 256


def theta_kernel(gate_ref, bounds_ref, a_ref, b_ref, start_ref, theta_ref, own_ref, image_ref):
    width = start_ref.shape[1]
    height = a_ref.shape[0]
    kept_right, kept_mid, first = bounds_ref[0], bounds_ref[1], bounds_ref[2]
    lane = lax.broadcasted_iota(jnp.int32, (height, CHUNK), 1)

    def mix(c, carry):
        offset = c * CHUNK
        inside = lane + offset < kept_right
        mixed = []
        for i in range(2):
            for j in range(2):
                columns = pl.ds(pl.multiple_of(j * width + offset, CHUNK), CHUNK)
                product = jnp.dot(
                    a_ref[:, i * width : (i + 1) * width],
                    b_ref[:, columns],
                    preferred_element_type=jnp.float32,
                )
                mixed.append(jnp.where(inside, product, 0.0))
        for o in range(2):
            for q in range(2):
                row = 4 * (2 * o + q)
                value = (
                    gate_ref[row] * mixed[0]
                    + gate_ref[row + 1] * mixed[1]
                    + gate_ref[row + 2] * mixed[2]
                    + gate_ref[row + 3] * mixed[3]
                )
                columns = pl.ds(pl.multiple_of(q * width + offset, CHUNK), CHUNK)
                theta_ref[o, :, columns] = value.astype(jnp.bfloat16)
        return carry

    lax.fori_loop(0, width // CHUNK, mix, 0)

    def image(c, carry):
        columns = pl.ds(pl.multiple_of(c * CHUNK, CHUNK), CHUNK)
        total = jnp.dot(
            theta_ref[first, :, :width], start_ref[0, :, columns], preferred_element_type=jnp.float32
        ) + jnp.dot(
            theta_ref[first, :, width:], start_ref[1, :, columns], preferred_element_type=jnp.float32
        )
        image_ref[:, columns] = jnp.where(lane + c * CHUNK < kept_mid, total, 0.0).astype(jnp.bfloat16)
        return carry

    lax.fori_loop(0, width // CHUNK, image, 0)

    def term(c, carry):
        columns = pl.ds(pl.multiple_of(c * CHUNK, CHUNK), CHUNK)
        own_ref[columns, :] = jnp.dot(
            turned(theta_ref[first, :, columns]), image_ref[...], preferred_element_type=jnp.float32
        ).astype(jnp.bfloat16)
        return carry

    lax.fori_loop(0, 2 * width // CHUNK, term, 0)


def theta_terms(gate, bounds, a_used, b_full, starts):
    height, wide = a_used.shape
    width = starts.shape[2]
    return pl.pallas_call(
        theta_kernel,
        out_shape=(
            jax.ShapeDtypeStruct((2, height, wide), jnp.bfloat16),
            jax.ShapeDtypeStruct((wide, width), jnp.bfloat16),
        ),
        in_specs=[pl.BlockSpec(memory_space=pltpu.SMEM)] * 2 + [pl.BlockSpec(memory_space=pltpu.VMEM)] * 3,
        out_specs=(pl.BlockSpec(memory_space=pltpu.VMEM),) * 2,
        scratch_shapes=[pltpu.VMEM((height, width), jnp.bfloat16)],
    )(gate, bounds, a_used, b_full, starts)


MESH = pl.DeviceIdType.MESH


class Links:
    def __init__(self, send_sem, recv_sem):
        self.chain, self.me = lax.axis_index("chain"), lax.axis_index("bond")
        self.core = self.chain % 2
        self.near = self.me + 1 - 2 * (self.me % 2)
        self.far = (self.me + 2) % 4
        self.across = 3 - self.me
        self.x, self.y, self.d = (self.chain, self.near), (self.chain, self.far), (self.chain, self.across)
        self.mate = (self.chain + 1 - 2 * self.core, self.me)
        self.send_sem, self.recv_sem, self.copies = send_sem, recv_sem, []

    def greet(self, others):
        barrier = pltpu.get_barrier_semaphore()
        for other in others:
            pl.semaphore_signal(barrier, inc=1, device_id=other, device_id_type=MESH)
        pl.semaphore_wait(barrier, len(others))

    def send(self, source, target, device):
        slot = len(self.copies)
        copy = pltpu.make_async_remote_copy(
            src_ref=source,
            dst_ref=target,
            send_sem=self.send_sem.at[slot],
            recv_sem=self.recv_sem.at[slot],
            device_id=device,
            device_id_type=MESH,
        )
        copy.start()
        self.copies.append(copy)
        return copy

    def spread(self, first_own, second_own, first, second):
        s0 = self.send(second_own, second(self.me), self.x)
        f0 = self.send(first_own, first(self.me), self.y)
        f1 = self.send(first_own, first(self.me), self.x)
        s1 = self.send(second_own, second(self.me), self.y)
        f0.wait_recv()
        f2 = self.send(first(self.far), first(self.far), self.x)
        late = [self.send(first(self.far), first(self.far), self.mate)]
        s0.wait_recv()
        s2 = self.send(second(self.near), second(self.near), self.y)
        late.append(self.send(second(self.near), second(self.near), self.mate))
        f1.wait_recv()
        late.append(self.send(first(self.near), first(self.near), self.mate))
        s1.wait_recv()
        late.append(self.send(second(self.far), second(self.far), self.mate))
        f2.wait_recv()
        late.append(self.send(first(self.across), first(self.across), self.mate))
        s2.wait_recv()
        late.append(self.send(second(self.across), second(self.across), self.mate))
        for copy in late:
            copy.wait_recv()

    def drain(self):
        for copy in self.copies:
            copy.wait_send()


def gather_kernel(b_ref, s_ref, b_out, s_out, send_sem, recv_sem, local_sem):
    links = Links(send_sem, recv_sem)
    links.greet((links.x, links.y, links.mate))
    core, me = links.core, links.me
    kept_b = pltpu.make_async_copy(b_ref, b_out.at[me], local_sem.at[0])
    kept_s = pltpu.make_async_copy(s_ref, s_out.at[core, me], local_sem.at[1])
    own = links.send(s_ref, s_out.at[core, me], links.mate)
    kept_b.start()
    kept_s.start()
    links.spread(
        b_ref.at[core], s_ref, lambda i: b_out.at[i, core], lambda i: s_out.at[core, i]
    )
    own.wait_recv()
    links.drain()
    kept_b.wait()
    kept_s.wait()


def gather_pair(b_rows, own_start):
    rows, wide = b_rows.shape
    width = own_start.shape[1]
    n = lax.axis_size("bond")
    b_full, starts = pl.pallas_call(
        gather_kernel,
        out_shape=(
            jax.ShapeDtypeStruct((n, 2, rows // 2, wide), b_rows.dtype),
            jax.ShapeDtypeStruct((2, n, rows, width), own_start.dtype),
        ),
        in_specs=[pl.BlockSpec(memory_space=pltpu.VMEM)] * 2,
        out_specs=(pl.BlockSpec(memory_space=pl.ANY),) * 2,
        scratch_shapes=[
            pltpu.SemaphoreType.DMA((13,)),
            pltpu.SemaphoreType.DMA((13,)),
            pltpu.SemaphoreType.DMA((2,)),
        ],
        compiler_params=pltpu.CompilerParams(collective_id=0, has_side_effects=True),
    )(b_rows.reshape(2, rows // 2, wide), own_start)
    return b_full.reshape(n * rows, wide), starts.reshape(2, n * rows, width)


def reduce_kernel(own_ref, out_ref, inc, acc, one, two, send_sem, recv_sem):
    links = Links(send_sem, recv_sem)
    links.greet((links.x, links.y, links.mate))
    core, me, near, far, across = links.core, links.me, links.near, links.far, links.across
    half = own_ref.shape[2] // 2
    low, high = pl.ds(0, half), pl.ds(half, half)
    order = (across, near, far, me)
    swaps = [links.send(own_ref.at[1 - core, i], inc.at[i], links.mate) for i in order]

    def merge(position):
        i = order[position]
        swaps[position].wait_recv()
        acc[i] = (own_ref[core, i].astype(jnp.float32) + inc[i].astype(jnp.float32)).astype(jnp.bfloat16)

    merge(0)
    x1 = links.send(acc.at[across, low], one.at[0, 1], links.x)
    y1 = links.send(acc.at[across, high], one.at[1, 1], links.y)
    merge(1)
    x0 = links.send(acc.at[near, low], one.at[0, 0], links.x)
    merge(2)
    y0 = links.send(acc.at[far, high], one.at[1, 0], links.y)
    merge(3)
    x1.wait_recv()
    two[2] = (acc[far, low].astype(jnp.float32) + one[0, 1].astype(jnp.float32)).astype(jnp.bfloat16)
    y2 = links.send(two.at[2], two.at[0], links.y)
    y1.wait_recv()
    two[3] = (acc[near, high].astype(jnp.float32) + one[1, 1].astype(jnp.float32)).astype(jnp.bfloat16)
    x2 = links.send(two.at[3], two.at[1], links.x)
    x0.wait_recv()
    y2.wait_recv()
    out_ref[core, me, low] = (
        acc[me, low].astype(jnp.float32) + one[0, 0].astype(jnp.float32) + two[0].astype(jnp.float32)
    ).astype(jnp.bfloat16)
    y0.wait_recv()
    x2.wait_recv()
    out_ref[core, me, high] = (
        acc[me, high].astype(jnp.float32) + one[1, 0].astype(jnp.float32) + two[1].astype(jnp.float32)
    ).astype(jnp.bfloat16)
    own = links.send(out_ref.at[core, me], out_ref.at[core, me], links.mate)
    links.spread(
        out_ref.at[core, me, low],
        out_ref.at[core, me, high],
        lambda i: out_ref.at[core, i, low],
        lambda i: out_ref.at[core, i, high],
    )
    own.wait_recv()
    links.drain()


def reduce_pair(own):
    total, width = own.shape
    n = lax.axis_size("bond")
    rows = total // (2 * n)
    whole = pl.pallas_call(
        reduce_kernel,
        out_shape=jax.ShapeDtypeStruct((2, n, rows, width), own.dtype),
        in_specs=[pl.BlockSpec(memory_space=pltpu.VMEM)],
        out_specs=pl.BlockSpec(memory_space=pltpu.VMEM),
        scratch_shapes=[
            pltpu.VMEM((n, rows, width), own.dtype),
            pltpu.VMEM((n, rows, width), own.dtype),
            pltpu.VMEM((2, 2, rows // 2, width), own.dtype),
            pltpu.VMEM((4, rows // 2, width), own.dtype),
            pltpu.SemaphoreType.DMA((23,)),
            pltpu.SemaphoreType.DMA((23,)),
        ],
        compiler_params=pltpu.CompilerParams(collective_id=1, has_side_effects=True),
    )(own.reshape(2, n, rows, width))
    return whole.reshape(total, width)


def total_kernel(value_ref, out_ref, held, send_sem, recv_sem):
    links = Links(send_sem, recv_sem)
    others = (links.x, links.y, links.d)
    links.greet(others)
    copies = [links.send(value_ref, held.at[i], other) for i, other in enumerate(others)]
    for copy in copies:
        copy.wait_recv()
    out_ref[...] = (value_ref[...] + held[2]) + (held[0] + held[1])
    links.drain()


def total_of(value):
    shape = (8, 128)
    return pl.pallas_call(
        total_kernel,
        out_shape=jax.ShapeDtypeStruct(shape, jnp.float32),
        in_specs=[pl.BlockSpec(memory_space=pltpu.VMEM)],
        out_specs=pl.BlockSpec(memory_space=pltpu.VMEM),
        scratch_shapes=[
            pltpu.VMEM((3,) + shape, jnp.float32),
            pltpu.SemaphoreType.DMA((3,)),
            pltpu.SemaphoreType.DMA((3,)),
        ],
        compiler_params=pltpu.CompilerParams(collective_id=2, has_side_effects=True),
    )(jnp.full(shape, value, jnp.float32))[:1, :1]


def local(sites, start, gates, bonds):
    bond_index = lax.axis_index("bond")
    chain_index = lax.axis_index("chain")
    rank_width = start.shape[2]
    local_rows = sites.shape[1]
    own_site = sites[0]
    own_start = start[0]
    is_left = chain_index % 2 == 0
    left_site = jnp.where(is_left, chain_index, chain_index - 1)
    bond_left = bonds[left_site]
    bond_mid = bonds[left_site + 1]
    bond_right = bonds[left_site + 2]
    columns = jnp.arange(rank_width)
    row_global = bond_index * local_rows + jnp.arange(local_rows)
    mid_keep = columns < bond_mid
    other_rows = partner(own_site, "chain", 0)
    a_rows = jnp.where(is_left, own_site, other_rows)
    b_rows = jnp.where(is_left, other_rows, own_site)
    square = lax.axis_size("bond") == 4
    if square:
        b_full, starts = gather_pair(b_rows, own_start)
    else:
        b_full = lax.all_gather(b_rows, "bond", axis=0, tiled=True)
        whole_start = lax.all_gather(own_start, "bond", axis=0, tiled=True)
        other_start = partner(whole_start, "chain", 0)
        starts = jnp.stack(
            [jnp.where(is_left, whole_start, other_start), jnp.where(is_left, other_start, whole_start)]
        )
    left_keep = (row_global < bond_left)[:, None] & jnp.tile(mid_keep, 2)[None, :]
    left_used = jnp.where(left_keep, a_rows, jnp.zeros((), jnp.bfloat16))
    bounds = jnp.stack([bond_right, bond_mid, jnp.where(is_left, 0, 1)]).astype(jnp.int32)
    thetas, own = theta_terms(gates[left_site], bounds, left_used, b_full, starts)
    if square:
        projected_all = reduce_pair(own)
    else:
        kept_half = jnp.where(is_left, 0, 1)
        half_rows = own.shape[0] // 2
        kept = lax.dynamic_slice_in_dim(own, kept_half * half_rows, half_rows, 0)
        given = lax.dynamic_slice_in_dim(own, (1 - kept_half) * half_rows, half_rows, 0)
        both = (kept.astype(jnp.float32) + partner(given, "chain", 0).astype(jnp.float32)).astype(jnp.bfloat16)
        summed = lax.psum_scatter(both, "bond", scatter_dimension=0, tiled=True)
        own_half = lax.all_gather(summed, "bond", axis=0, tiled=True)
        other_half = partner(own_half, "chain", 0)
        projected_all = jnp.concatenate(
            [jnp.where(is_left, own_half, other_half), jnp.where(is_left, other_half, own_half)], axis=0
        )
    inverse = factor_inverse(bounds, projected_all)

    def left_rows():
        reduced = jnp.dot(
            thetas.reshape(2 * local_rows, -1), projected_all, preferred_element_type=jnp.float32
        )
        upper = lax.dot_general(
            reduced,
            inverse,
            (((1,), (1,)), ((), ())),
            precision=lax.Precision.HIGH,
            preferred_element_type=jnp.float32,
        )
        joined = jnp.concatenate([upper[:local_rows], upper[local_rows:]], axis=1)
        return joined, jnp.sum(joined * joined)

    def right_rows():
        block = lax.dynamic_slice_in_dim(inverse, bond_index * local_rows, local_rows, 0)
        basis_rows = lax.dot_general(
            block,
            projected_all.astype(jnp.float32),
            (((1,), (1,)), ((), ())),
            precision=lax.Precision.HIGH,
            preferred_element_type=jnp.float32,
        )
        return basis_rows, jnp.float32(0.0)

    rows, squares = lax.cond(is_left, left_rows, right_rows)
    sum_squares = total_of(squares) if square else lax.psum(squares, "bond")
    mean_square = (
        sum_squares / (2.0 * bond_left.astype(jnp.float32) * bond_mid.astype(jnp.float32)) + 1e-06
    )
    factor = jnp.where(
        jnp.full(jnp.shape(mean_square), is_left), lax.rsqrt(mean_square), jnp.sqrt(2.0 * bond_right.astype(jnp.float32))
    )
    return (rows * factor)[None]


def solution(mesh):
    placed = (P("chain", "bond", None), P("chain", "bond", None), P(), P())
    return jax.shard_map(
        local, mesh=mesh, in_specs=placed, out_specs=P("chain", "bond", None), check_vma=False
    )
```

profile of v0, /device:TPU:0, one launch (start us, length us, event | category | flops | bytes accessed | tf_op | source)
XLA Modules:
  0.0 186.0 jit_solution(8413071033080568387)
XLA Ops:
  0.0 0.0 copy-start
  0.0 0.5 collective-permute-start
  0.5 1.4 fusion.4
  3.8 0.6 iota_compare_fusion
  4.5 0.6 add_compare_fusion
  5.1 1.9 %pad_add_fusion.bounds_ref = s32[3]{0:T(128)} fusion(s32[1]{0:T(128)} %bitcast.1, s32[1]{0:T(128)} %get-tuple-element.43, s32[1]{0:T(128)} %get-tuple-element.42), kind=kLoop, calls=%fused_computation.10 | loop fusion | flops 6 | bytes 24 | tf_op jit(solution)/shard_map/stack | solution.py:446
  7.1 0.0 copy-done
  7.1 0.5 dynamic-slice_bitcast_fusion.gate_ref
  7.6 0.0 collective-permute-done
  7.6 3.3 %broadcast_select_fusion = (bf16[256,2048]{1,0:T(8,128)(2,1)}, bf16[256,2048]{1,0:T(8,128)(2,1)}) fusion(bf16[256,2048]{1,0:T(8,128)(2,1)S(1)} %collective-permute-done, pred[]{:T(512)} %eq.5, bf16[1,256,2048]{2,1,0:T(8,128)(2,1)} %param.6, pred[2048]{0:T(1024)(128)(4,1)S(1)} %and.24, pred[256]{0:T(512)(128)(4,1)S(1)} %add_compare_fusion), kind=kLoop, calls=%fused_computation.7 | loop fusion | flops 2097152 | bytes 4196609 | tf_op jit(solution)/shard_map/jit(_where)/select_n | solution.py:433
  10.9 43.1 %shard_map.46 = (bf16[4,2,128,2048]{3,2,1,0:T(8,128)(2,1)}, bf16[2,4,256,1024]{3,2,1,0:T(8,128)(2,1)}) custom-call(bf16[2,128,2048]{2,1,0:T(8,128)(2,1)} %bitcast.32, bf16[256,1024]{1,0:T(8,128)(2,1)} %bitcast.34), custom_call_target="tpu_custom_call" | custom-call | tf_op jit(solution)/shard_map/pallas_call | solution.py:300
  54.1 14.7 %shard_map.47 = (bf16[2,256,2048]{2,1,0:T(8,128)(2,1)}, bf16[2048,1024]{1,0:T(8,128)(2,1)}) custom-call(f32[16]{0:T(128)} %dynamic-slice_bitcast_fusion.gate_ref, s32[3]{0:T(128)} %pad_add_fusion.bounds_ref, bf16[256,2048]{1,0:T(8,128)(2,1)} %get-tuple-element.40.a_ref, bf16[1024,2048]{1,0:T(8,128)(2,1)} %bitcast.29, bf16[2,1024,1024]{2,1,0:T(8,128)(2,1)} %bitcast.30), custom_call_target="tpu_custom_call" | custom-call | tf_op jit(solution)/shard_map/pallas_call | solution.py:205
  68.7 46.1 %shard_map.48 = bf16[2,4,256,1024]{3,2,1,0:T(8,128)(2,1)} custom-call(bf16[2,4,256,1024]{3,2,1,0:T(8,128)(2,1)} %bitcast.31), custom_call_target="tpu_custom_call" | custom-call | tf_op jit(solution)/shard_map/pallas_call | solution.py:371
  114.9 50.1 %shard_map.49 = f32[1024,1024]{1,0:T(8,128)} custom-call(s32[3]{0:T(128)} %pad_add_fusion.bounds_ref, bf16[2048,1024]{1,0:T(8,128)(2,1)} %bitcast.26), custom_call_target="tpu_custom_call" | custom-call | tf_op jit(solution)/shard_map/pallas_call | solution.py:134
  165.0 11.1 %conditional.1 = (f32[256,2048]{1,0:T(8,128)S(1)}, f32[]{:T(128)}) conditional(s32[]{:T(128)} %convert_element_type.14, (s32[]{:T(128)}, f32[1024,1024]{1,0:T(8,128)}, bf16[2048,1024]{1,0:T(8,128)(2,1)}) %tuple.22, (bf16[2,256,2048]{2,1,0:T(8,128)(2,1)}, bf16[2048,1024]{1,0:T(8,128)(2,1)}, f32[1024,1024]{1,0:T(8,128)}) %tuple.23), branch_computations={%region_0.1_spmd, %region_1.3_spmd} | conditional | flops 5370281984 | bytes 41943088 | solution.py:489
  165.0 0.0 copy-start.1
  165.0 5.3 %fusion.5 = f32[512,1024]{1,0:T(8,128)S(1)} fusion(bf16[512,2048]{1,0:T(8,128)(2,1)} %bitcast.35, bf16[2048,1024]{1,0:T(8,128)(2,1)} %get-tuple-element.21), kind=kOutput, calls=%fused_computation.14 | convolution fusion | flops 2147483648 | bytes 8388608 | tf_op jit(solution)/shard_map/cond/branch_1_fun/dot_general | solution.py:465
  170.3 0.0 copy-done.1
  170.3 3.7 %fusion.6 = f32[512,1024]{1,0:T(8,128)S(1)} fusion(f32[512,1024]{1,0:T(8,128)S(1)} %fusion.5, f32[1024,1024]{1,0:T(8,128)S(1)} %copy-done.1), kind=kOutput, calls=%fused_computation.15 | convolution fusion | flops 3221225472 | bytes 8388608 | tf_op jit(solution)/shard_map/cond/branch_1_fun/dot_general | solution.py:468
  174.1 0.1 fusion.3
  174.2 1.2 multiply_reduce_fusion
  176.1 0.6 broadcast_in_dim.20.value_ref
  176.7 5.9 %shard_map.50 = f32[8,128]{1,0:T(8,128)} custom-call(f32[8,128]{1,0:T(8,128)} %broadcast_in_dim.20.value_ref), custom_call_target="tpu_custom_call" | custom-call | tf_op jit(solution)/shard_map/pallas_call | solution.py:402
  182.6 1.2 slice.9
  184.5 1.5 multiply_bitcast_fusion
  (2 shorter events, 0.0 us)
Async XLA Ops:
  0.0 7.1 %copy-start = (f32[8,16]{1,0:T(8,128)S(1)}, f32[8,16]{1,0:T(8,128)}, u32[]{:S(2)}) copy-start(f32[8,16]{1,0:T(8,128)} %param.8) | copy-start | bytes 1540
  0.0 7.6 %collective-permute-start = (bf16[256,2048]{1,0:T(8,128)(2,1)}, bf16[256,2048]{1,0:T(8,128)(2,1)S(1)}, u32[]{:S(2)}, u32[]{:S(2)}) collective-permute-start(bf16[256,2048]{1,0:T(8,128)(2,1)} %bitcast.33), channel_id=1, source_target_pairs={{0,4},{4,0},{8,12},{12,8},{16,20},{20,16},{24,28},{28,24},{1,5},{5... | collective-permute-start | bytes 3145736 | tf_op jit(solution)/shard_map/ppermute | solution.py:14
  165.0 5.3 %copy-start.1 = (f32[1024,1024]{1,0:T(8,128)S(1)}, f32[1024,1024]{1,0:T(8,128)}, u32[]{:S(2)}) copy-start(f32[1024,1024]{1,0:T(8,128)} %get-tuple-element.22) | copy-start | bytes 12582916 | tf_op jit(solution)/shard_map/cond
where the time goes:
time: 186 us
  Pallas kernels  160 us (86%)
  other arithmetic  9.2 us (5%)
  matrix products  9.01 us (5%)
  local copies, waits for them, and re-layouts  3.9 us (2%)
  between operations  2.7 us (1%)
    pallas_call x1, Pallas kernels, factor_inverse(): pl.pallas_call(factor_kernel, out_shape=jax.ShapeDtypeStruct((size, size)...  50.1 us
    pallas_call x1, Pallas kernels, reduce_pair(): pl.pallas_call(reduce_kernel, out_shape=jax.ShapeDtypeStruct((2, n, rows,...  46.1 us
    pallas_call x1, Pallas kernels, gather_pair(): pl.pallas_call(gather_kernel, out_shape=(jax.ShapeDtypeStruct((n, 2, rows...  43.1 us
    pallas_call x1, Pallas kernels, theta_terms(): pl.pallas_call(theta_kernel, out_shape=(jax.ShapeDtypeStruct((2, height,...  14.7 us
    pallas_call x1, Pallas kernels, total_of(): pl.pallas_call(total_kernel, out_shape=jax.ShapeDtypeStruct(shape, jnp.fl...  5.93 us
    dot_general x1, matrix products, left_rows(): jnp.dot(thetas.reshape(2 * local_rows, -1), projected_all, preferred_elem...  5.29 us
  transfers between devices with their start and end apart: 1, of which 0 were waited for; matrix products, arithmetic and copies ran while one was open for 3% of the time, Pallas kernels for 0%

commit v1 on v0

--- a/solution.py
+++ b/solution.py
@@ -19,50 +19,101 @@
     return high, (x - high.astype(jnp.float32)).astype(jnp.bfloat16)
 
 
-def diagonal_inverse(tile):
+def lane_of(x, j):
+    return jnp.broadcast_to(x[:, j : j + 1], (SUB, BLOCK))
+
+
+def row_of(x, j):
+    return jnp.broadcast_to(x[j : j + 1, :], (SUB, BLOCK))
+
+
+def eliminate(rows, first):
     lane = lax.broadcasted_iota(jnp.int32, (SUB, BLOCK), 1)
     sub = lax.broadcasted_iota(jnp.int32, (SUB, BLOCK), 0)
-    count = BLOCK // SUB
-    rows = [tile[i * SUB : (i + 1) * SUB, :] for i in range(count)]
-    full = (SUB, BLOCK)
-    for b in range(count):
-        base = b * SUB
-        cols = [jnp.broadcast_to(rows[b][:, base + j : base + j + 1], full) for j in range(SUB)]
-        current = rows[b]
-        scale = jnp.zeros(full, jnp.float32)
-        inverses, uppers, finals = [], {}, []
-        for j in range(SUB):
-            pivot = jnp.broadcast_to(cols[j][j : j + 1, :], full)
-            inv = 1.0 / pivot
-            inverses.append(inv)
-            scale = jnp.where(sub == j, pivot, scale)
-            m = jnp.where(sub > j, cols[j] * inv, 0.0)
-            for k in range(j + 1, SUB):
-                uppers[j, k] = jnp.broadcast_to(cols[k][j : j + 1, :], full)
-                cols[k] = cols[k] - m * uppers[j, k]
-            row = jnp.broadcast_to(current[j : j + 1, :], full)
-            row = jnp.where(lane == base + j, 1.0, row)
-            finals.append(jnp.where((lane > base + j) & (lane < base + SUB), 0.0, row))
-            current = jnp.where((lane == base + j) & (sub >= j), jnp.where(sub == j, 1.0, 0.0), current) - m * row
-        inside = (lane >= base) & (lane < base + SUB)
-        for i in range(b + 1, count):
-            held = [jnp.broadcast_to(rows[i][:, base + j : base + j + 1], full) for j in range(SUB)]
-            fresh = jnp.where(inside, 0.0, rows[i])
-            for j in range(SUB):
-                c = held[j] * inverses[j]
-                for k in range(j + 1, SUB):
-                    held[k] = held[k] - c * uppers[j, k]
-                fresh = fresh - c * finals[j]
-            rows[i] = fresh
-        rows[b] = jnp.where(lane <= base + sub, current * lax.rsqrt(scale), 0.0)
-    return jnp.concatenate(rows, axis=0)
+    rows = list(rows)
+    for t in range(0, len(rows), 2):
+        base = first + t * SUB
+        inside = (lane >= base) & (lane < base + 2 * SUB)
+        columns = (
+            [lane_of(rows[t], base + j) for j in range(SUB)],
+            [lane_of(rows[t + 1], base + j) for j in range(2 * SUB)],
+        )
+        below = range(t + 2, len(rows))
+        held = {i: [lane_of(rows[i], base + j) for j in range(2 * SUB)] for i in below}
+        current = [
+            jnp.where(inside, jnp.where(lane == base + sub + h * SUB, 1.0, 0.0), rows[t + h]) for h in range(2)
+        ]
+        fresh = {i: jnp.where(inside, 0.0, rows[i]) for i in below}
+        pivots = [jnp.ones((SUB, BLOCK), jnp.float32)] * 2
+        for j in range(0, 2 * SUB, 2):
+            half, local = j // SUB, j % SUB
+            source = columns[half]
+            a, b, c = row_of(source[j], local), row_of(source[j], local + 1), row_of(source[j + 1], local + 1)
+            inverses = [1.0 / a, a * (1.0 / (a * c - b * b))]
+            values = [a, c - b * b * inverses[0]]
+            for q in (j, j + 1):
+                inv, at = inverses[q - j], q % SUB
+                pivots[half] = jnp.where(sub == at, values[q - j], pivots[half])
+                uppers = {k: row_of(columns[k // SUB][q], k % SUB) for k in range(q + 1, 2 * SUB)}
+                row = row_of(current[half], at)
+                for h in range(half, 2):
+                    m = columns[h][q] * inv
+                    for k in range(q + 1, (h + 1) * SUB):
+                        columns[h][k] = columns[h][k] - m * uppers[k]
+                    current[h] = current[h] - (jnp.where(sub > at, m, 0.0) if h == half else m) * row
+                for i in below:
+                    m = held[i][q] * inv
+                    for k in range(q + 1, 2 * SUB):
+                        held[i][k] = held[i][k] - m * uppers[k]
+                    fresh[i] = fresh[i] - m * row
+        for h in range(2):
+            rows[t + h] = current[h] * lax.rsqrt(pivots[h])
+        for i in below:
+            rows[i] = fresh[i]
+    return rows
+
+
+def threefold(x):
+    high, low = halves(x)
+    return jnp.concatenate([high, low, high], axis=0)
+
+
+def threewide(x):
+    high, low = halves(x)
+    return jnp.concatenate([high, high, low], axis=1)
+
+
+GROUP = 64
+
+
+def diagonal_inverse(tile):
+    part = GROUP // SUB
+    rows = [tile[i * SUB : (i + 1) * SUB, :] for i in range(BLOCK // SUB)]
+    for g in range(0, len(rows), part):
+        rows[g : g + part] = eliminate(rows[g : g + part], g * SUB)
+        if g + part < len(rows):
+            done = jnp.concatenate(rows[g : g + part], axis=0)
+            line = lax.broadcasted_iota(jnp.int32, done.shape, 0) + g * SUB
+            lane = lax.broadcasted_iota(jnp.int32, done.shape, 1)
+            right = jnp.where((lane > line) & (lane < (g + part) * SUB), 0.0, done)
+            left = done.T[(g + part) * SUB :, :]
+            update = jnp.dot(threewide(left), threefold(right), preferred_element_type=jnp.float32)
+            lane = lax.broadcasted_iota(jnp.int32, (SUB, BLOCK), 1)
+            inside = (lane >= g * SUB) & (lane < (g + part) * SUB)
+            for i in range(g + part, len(rows)):
+                there = slice((i - g - part) * SUB, (i - g - part + 1) * SUB)
+                rows[i] = jnp.where(inside, 0.0, rows[i]) - update[there, :]
+    whole = jnp.concatenate(rows, axis=0)
+    line = lax.broadcasted_iota(jnp.int32, whole.shape, 0)
+    lane = lax.broadcasted_iota(jnp.int32, whole.shape, 1)
+    return jnp.where(lane <= line, whole, 0.0)
 
 
 def turned(x):
     return x.astype(jnp.float32).T.astype(x.dtype)
 
 
-def factor_kernel(bounds_ref, rows_ref, out_ref, right_ref):
+def factor_kernel(bounds_ref, rows_ref, out_ref, tile_ref, inverse_ref):
     size = out_ref.shape[0]
     count = size // BLOCK
     wide = 2 * BLOCK
@@ -80,53 +131,48 @@
         diagonal = diagonal + jnp.where(eye, out_ref[here, here], 0.0)
     trace = jnp.sum(jnp.sum(diagonal, axis=0, keepdims=True), axis=1, keepdims=True)
     ridge = ridge_ratio * trace / jnp.full((1, 1), kept, jnp.int32).astype(jnp.float32)
+    unit = 1.0 / ridge
+    root = lax.rsqrt(ridge)
     for i in range(count):
         here = slice(i * BLOCK, (i + 1) * BLOCK)
-        added = jnp.where(across + i * BLOCK < kept, jnp.broadcast_to(ridge, eye.shape), 1.0)
-        out_ref[here, here] = out_ref[here, here] + jnp.where(eye, added, 0.0)
+        out_ref[here, here] = out_ref[here, here] + jnp.where(eye, ridge, 0.0)
+    tile_ref[...] = out_ref[0:BLOCK, 0:BLOCK] * unit
+    inverse_ref[...] = jnp.zeros_like(inverse_ref)
+
+    def finish(k, live):
+        here = pl.ds(pl.multiple_of(k * BLOCK, BLOCK), BLOCK)
+        inverse = inverse_ref[...]
+        done = jnp.dot(threewide(inverse), threefold(out_ref[here, :]), preferred_element_type=jnp.float32)
+        column = lax.broadcasted_iota(jnp.int32, (BLOCK, size), 1)
+        own = (column >= k * BLOCK) & (column < (k + 1) * BLOCK)
+        done = jnp.where(own, jnp.concatenate([inverse] * count, axis=1), done)
+        out_ref[here, :] = jnp.where(live, jnp.where(column < (k + 1) * BLOCK, done, 0.0), out_ref[here, :])
+        return done, own
 
     def panel(k, carry):
+        before = jnp.maximum(k - 1, 0)
+        inverse = diagonal_inverse(tile_ref[...]) * root
+        done, own = finish(before, k > 0)
+        right = threefold(done)
+        for i in range(1, count):
+            there = slice(i * BLOCK, (i + 1) * BLOCK)
+            left = threewide(done[:, there].T)
+            left = jnp.where(i >= k, left, jnp.zeros((), left.dtype))
+            left = jnp.where(k > 0, left, jnp.zeros((), left.dtype))
+            kept_rows = jnp.where((i >= k) & (k > 0) & own, 0.0, out_ref[there, :])
+            out_ref[there, :] = kept_rows - jnp.dot(left, right, preferred_element_type=jnp.float32)
+        inverse_ref[...] = inverse
         here = pl.ds(pl.multiple_of(k * BLOCK, BLOCK), BLOCK)
-        inverse = diagonal_inverse(out_ref[here, here])
-        inv_high, inv_low = halves(inverse)
-        row_high, row_low = halves(out_ref[here, :])
-        out_ref[here, :] = jnp.dot(
-            jnp.concatenate([inv_high, inv_high, inv_low], axis=1),
-            jnp.concatenate([row_high, row_low, row_high], axis=0),
-            preferred_element_type=jnp.float32,
-        )
-        out_ref[here, here] = inverse
-        high, low = halves(out_ref[here, :])
-        right_ref[0:BLOCK, :] = high
-        right_ref[BLOCK : 2 * BLOCK, :] = low
-        right_ref[2 * BLOCK : 3 * BLOCK, :] = high
-
-        def trailing(first, height):
-            there = pl.ds(pl.multiple_of(first * BLOCK, BLOCK), height)
-            left_high, left_low = halves(out_ref[here, there].T)
-            out_ref[there, here] = jnp.zeros((height, BLOCK), jnp.float32)
-            out_ref[there, :] = out_ref[there, :] - jnp.dot(
-                jnp.concatenate([left_high, left_high, left_low], axis=1),
-                right_ref[...],
-                preferred_element_type=jnp.float32,
-            )
-
-        odd = (count - 1 - k) % 2
-
-        @pl.when(odd == 1)
-        def _():
-            trailing(k + 1, BLOCK)
-
-        def pair(i, inner):
-            trailing(k + 1 + odd + 2 * i, wide)
-            return inner
-
-        lax.fori_loop(0, (count - 1 - k) // 2, pair, 0)
-        column = lax.broadcasted_iota(jnp.int32, (BLOCK, size), 1)
-        out_ref[here, :] = jnp.where(column < (k + 1) * BLOCK, out_ref[here, :], 0.0)
+        after = pl.ds(pl.multiple_of(jnp.minimum(k + 1, count - 1) * BLOCK, BLOCK), BLOCK)
+        across_next = jnp.dot(threewide(inverse), threefold(out_ref[here, after]), preferred_element_type=jnp.float32)
+        tile_ref[...] = unit * (
+            out_ref[after, after]
+            - jnp.dot(threewide(across_next.T), threefold(across_next), preferred_element_type=jnp.float32)
+        )
         return carry
 
     lax.fori_loop(0, count, panel, 0)
+    finish(count - 1, kept > 0)
 
 
 def factor_inverse(bounds, rows):
@@ -136,7 +182,7 @@
         out_shape=jax.ShapeDtypeStruct((size, size), jnp.float32),
         in_specs=[pl.BlockSpec(memory_space=pltpu.SMEM), pl.BlockSpec(memory_space=pltpu.VMEM)],
         out_specs=pl.BlockSpec(memory_space=pltpu.VMEM),
-        scratch_shapes=[pltpu.VMEM((3 * BLOCK, size), jnp.bfloat16)],
+        scratch_shapes=[pltpu.VMEM((BLOCK, BLOCK), jnp.float32)] * 2,
     )(bounds, rows)
 
 

time: 186 us -> 174 us (0.935)
  Pallas kernels: 160 us -> 147 us
    pallas_call x1, Pallas kernels: 50.1 us -> 37.5 us  [factor_inverse(): pl.pallas_call(factor_kernel, out_shape=jax.ShapeDtypeStruct((size, size)...]
where the time goes in v1:
time: 174 us; the launch traced here: 173 us
  Pallas kernels  147 us (84%)
  other arithmetic  9.2 us (5%)
  matrix products  9.01 us (5%)
  local copies, waits for them, and re-layouts  3.9 us (2%)
  between operations  2.7 us (2%)
    pallas_call x1, Pallas kernels, reduce_pair(): pl.pallas_call(reduce_kernel, out_shape=jax.ShapeDtypeStruct((2, n, rows,...  46.1 us
    pallas_call x1, Pallas kernels, gather_pair(): pl.pallas_call(gather_kernel, out_shape=(jax.ShapeDtypeStruct((n, 2, rows...  43.1 us
    pallas_call x1, Pallas kernels, factor_inverse(): pl.pallas_call(factor_kernel, out_shape=jax.ShapeDtypeStruct((size, size)...  37.5 us
    pallas_call x1, Pallas kernels, theta_terms(): pl.pallas_call(theta_kernel, out_shape=(jax.ShapeDtypeStruct((2, height,...  14.7 us
    pallas_call x1, Pallas kernels, total_of(): pl.pallas_call(total_kernel, out_shape=jax.ShapeDtypeStruct(shape, jnp.fl...  5.91 us
    dot_general x1, matrix products, left_rows(): jnp.dot(thetas.reshape(2 * local_rows, -1), projected_all, preferred_elem...  5.29 us
    dot_general x1, matrix products, left_rows(): lax.dot_general(reduced, inverse, (((1,), (1,)), ((), ())), precision=lax...  3.72 us
  transfers between devices with their start and end apart: 1, of which 0 were waited for; matrix products, arithmetic and copies ran while one was open for 3% of the time, Pallas kernels for 0%

profile of v1, /device:TPU:0, one launch (start us, length us, event | category | flops | bytes accessed | tf_op | source)
XLA Modules:
  0.0 173.4 jit_solution(9182557919514012273)
XLA Ops:
  0.0 0.0 copy-start
  0.0 0.5 collective-permute-start
  0.5 1.4 fusion.4
  3.8 0.6 iota_compare_fusion
  4.5 0.6 add_compare_fusion
  5.1 1.9 %pad_add_fusion.bounds_ref = s32[3]{0:T(128)} fusion(s32[1]{0:T(128)} %bitcast.1, s32[1]{0:T(128)} %get-tuple-element.43, s32[1]{0:T(128)} %get-tuple-element.42), kind=kLoop, calls=%fused_computation.10 | loop fusion | flops 6 | bytes 24 | tf_op jit(solution)/shard_map/stack | solution.py:492
  7.1 0.0 copy-done
  7.1 0.5 dynamic-slice_bitcast_fusion.gate_ref
  7.6 0.0 collective-permute-done
  7.6 3.3 %broadcast_select_fusion = (bf16[256,2048]{1,0:T(8,128)(2,1)}, bf16[256,2048]{1,0:T(8,128)(2,1)}) fusion(bf16[256,2048]{1,0:T(8,128)(2,1)S(1)} %collective-permute-done, pred[]{:T(512)} %eq.5, bf16[1,256,2048]{2,1,0:T(8,128)(2,1)} %param.6, pred[2048]{0:T(1024)(128)(4,1)S(1)} %and.24, pred[256]{0:T(512)(128)(4,1)S(1)} %add_compare_fusion), kind=kLoop, calls=%fused_computation.7 | loop fusion | flops 2097152 | bytes 4196609 | tf_op jit(solution)/shard_map/jit(_where)/select_n | solution.py:479
  10.9 43.1 %shard_map.46 = (bf16[4,2,128,2048]{3,2,1,0:T(8,128)(2,1)}, bf16[2,4,256,1024]{3,2,1,0:T(8,128)(2,1)}) custom-call(bf16[2,128,2048]{2,1,0:T(8,128)(2,1)} %bitcast.32, bf16[256,1024]{1,0:T(8,128)(2,1)} %bitcast.34), custom_call_target="tpu_custom_call" | custom-call | tf_op jit(solution)/shard_map/pallas_call | solution.py:346
  54.1 14.7 %shard_map.47 = (bf16[2,256,2048]{2,1,0:T(8,128)(2,1)}, bf16[2048,1024]{1,0:T(8,128)(2,1)}) custom-call(f32[16]{0:T(128)} %dynamic-slice_bitcast_fusion.gate_ref, s32[3]{0:T(128)} %pad_add_fusion.bounds_ref, bf16[256,2048]{1,0:T(8,128)(2,1)} %get-tuple-element.40.a_ref, bf16[1024,2048]{1,0:T(8,128)(2,1)} %bitcast.29, bf16[2,1024,1024]{2,1,0:T(8,128)(2,1)} %bitcast.30), custom_call_target="tpu_custom_call" | custom-call | tf_op jit(solution)/shard_map/pallas_call | solution.py:251
  68.7 46.1 %shard_map.48 = bf16[2,4,256,1024]{3,2,1,0:T(8,128)(2,1)} custom-call(bf16[2,4,256,1024]{3,2,1,0:T(8,128)(2,1)} %bitcast.31), custom_call_target="tpu_custom_call" | custom-call | tf_op jit(solution)/shard_map/pallas_call | solution.py:417
  114.9 37.5 %shard_map.49 = f32[1024,1024]{1,0:T(8,128)} custom-call(s32[3]{0:T(128)} %pad_add_fusion.bounds_ref, bf16[2048,1024]{1,0:T(8,128)(2,1)} %bitcast.26), custom_call_target="tpu_custom_call" | custom-call | tf_op jit(solution)/shard_map/pallas_call | solution.py:180
  152.4 11.1 %conditional.1 = (f32[256,2048]{1,0:T(8,128)S(1)}, f32[]{:T(128)}) conditional(s32[]{:T(128)} %convert_element_type.14, (s32[]{:T(128)}, f32[1024,1024]{1,0:T(8,128)}, bf16[2048,1024]{1,0:T(8,128)(2,1)}) %tuple.22, (bf16[2,256,2048]{2,1,0:T(8,128)(2,1)}, bf16[2048,1024]{1,0:T(8,128)(2,1)}, f32[1024,1024]{1,0:T(8,128)}) %tuple.23), branch_computations={%region_0.1_spmd, %region_1.3_spmd} | conditional | flops 5370281984 | bytes 41943088 | solution.py:535
  152.4 0.0 copy-start.1
  152.4 5.3 %fusion.5 = f32[512,1024]{1,0:T(8,128)S(1)} fusion(bf16[512,2048]{1,0:T(8,128)(2,1)} %bitcast.35, bf16[2048,1024]{1,0:T(8,128)(2,1)} %get-tuple-element.21), kind=kOutput, calls=%fused_computation.14 | convolution fusion | flops 2147483648 | bytes 8388608 | tf_op jit(solution)/shard_map/cond/branch_1_fun/dot_general | solution.py:511
  157.7 0.0 copy-done.1
  157.7 3.7 %fusion.6 = f32[512,1024]{1,0:T(8,128)S(1)} fusion(f32[512,1024]{1,0:T(8,128)S(1)} %fusion.5, f32[1024,1024]{1,0:T(8,128)S(1)} %copy-done.1), kind=kOutput, calls=%fused_computation.15 | convolution fusion | flops 3221225472 | bytes 8388608 | tf_op jit(solution)/shard_map/cond/branch_1_fun/dot_general | solution.py:514
  161.5 0.1 fusion.3
  161.6 1.2 multiply_reduce_fusion
  163.5 0.6 broadcast_in_dim.20.value_ref
  164.1 5.9 %shard_map.50 = f32[8,128]{1,0:T(8,128)} custom-call(f32[8,128]{1,0:T(8,128)} %broadcast_in_dim.20.value_ref), custom_call_target="tpu_custom_call" | custom-call | tf_op jit(solution)/shard_map/pallas_call | solution.py:448
  170.0 1.2 slice.9
  171.9 1.5 multiply_bitcast_fusion
  (2 shorter events, 0.0 us)
Async XLA Ops:
  0.0 7.1 %copy-start = (f32[8,16]{1,0:T(8,128)S(1)}, f32[8,16]{1,0:T(8,128)}, u32[]{:S(2)}) copy-start(f32[8,16]{1,0:T(8,128)} %param.8) | copy-start | bytes 1540
  0.0 7.6 %collective-permute-start = (bf16[256,2048]{1,0:T(8,128)(2,1)}, bf16[256,2048]{1,0:T(8,128)(2,1)S(1)}, u32[]{:S(2)}, u32[]{:S(2)}) collective-permute-start(bf16[256,2048]{1,0:T(8,128)(2,1)} %bitcast.33), channel_id=1, source_target_pairs={{0,4},{4,0},{8,12},{12,8},{16,20},{20,16},{24,28},{28,24},{1,5},{5... | collective-permute-start | bytes 3145736 | tf_op jit(solution)/shard_map/ppermute | solution.py:14
  152.4 5.3 %copy-start.1 = (f32[1024,1024]{1,0:T(8,128)S(1)}, f32[1024,1024]{1,0:T(8,128)}, u32[]{:S(2)}) copy-start(f32[1024,1024]{1,0:T(8,128)} %get-tuple-element.22) | copy-start | bytes 12582916 | tf_op jit(solution)/shard_map/cond

commit v2 on v1

--- a/solution.py
+++ b/solution.py
@@ -113,15 +113,10 @@
     return x.astype(jnp.float32).T.astype(x.dtype)
 
 
-def factor_kernel(bounds_ref, rows_ref, out_ref, tile_ref, inverse_ref):
+def factor_kernel(bounds_ref, gram_ref, out_ref, tile_ref, inverse_ref):
     size = out_ref.shape[0]
     count = size // BLOCK
-    wide = 2 * BLOCK
-    for i in range(size // wide):
-        left = turned(rows_ref[:, i * wide : (i + 1) * wide])
-        out_ref[i * wide : (i + 1) * wide, i * wide :] = jnp.dot(
-            left, rows_ref[:, i * wide :], preferred_element_type=jnp.float32
-        )
+    out_ref[...] = gram_ref[...]
     across = lax.broadcasted_iota(jnp.int32, (BLOCK, BLOCK), 1)
     eye = lax.broadcasted_iota(jnp.int32, (BLOCK, BLOCK), 0) == across
     kept = bounds_ref[1]
@@ -175,15 +170,15 @@
     finish(count - 1, kept > 0)
 
 
-def factor_inverse(bounds, rows):
-    size = rows.shape[1]
+def factor_inverse(bounds, gram):
+    size = gram.shape[1]
     return pl.pallas_call(
         factor_kernel,
         out_shape=jax.ShapeDtypeStruct((size, size), jnp.float32),
         in_specs=[pl.BlockSpec(memory_space=pltpu.SMEM), pl.BlockSpec(memory_space=pltpu.VMEM)],
         out_specs=pl.BlockSpec(memory_space=pltpu.VMEM),
         scratch_shapes=[pltpu.VMEM((BLOCK, BLOCK), jnp.float32)] * 2,
-    )(bounds, rows)
+    )(bounds, gram)
 
 
 CHUNK = 256
@@ -294,142 +289,389 @@
         self.copies.append(copy)
         return copy
 
-    def spread(self, first_own, second_own, first, second):
-        s0 = self.send(second_own, second(self.me), self.x)
-        f0 = self.send(first_own, first(self.me), self.y)
-        f1 = self.send(first_own, first(self.me), self.x)
-        s1 = self.send(second_own, second(self.me), self.y)
-        f0.wait_recv()
-        f2 = self.send(first(self.far), first(self.far), self.x)
-        late = [self.send(first(self.far), first(self.far), self.mate)]
-        s0.wait_recv()
-        s2 = self.send(second(self.near), second(self.near), self.y)
-        late.append(self.send(second(self.near), second(self.near), self.mate))
-        f1.wait_recv()
-        late.append(self.send(first(self.near), first(self.near), self.mate))
-        s1.wait_recv()
-        late.append(self.send(second(self.far), second(self.far), self.mate))
-        f2.wait_recv()
-        late.append(self.send(first(self.across), first(self.across), self.mate))
-        s2.wait_recv()
-        late.append(self.send(second(self.across), second(self.across), self.mate))
-        for copy in late:
-            copy.wait_recv()
-
     def drain(self):
         for copy in self.copies:
             copy.wait_send()
 
 
-def gather_kernel(b_ref, s_ref, b_out, s_out, send_sem, recv_sem, local_sem):
-    links = Links(send_sem, recv_sem)
-    links.greet((links.x, links.y, links.mate))
-    core, me = links.core, links.me
-    kept_b = pltpu.make_async_copy(b_ref, b_out.at[me], local_sem.at[0])
-    kept_s = pltpu.make_async_copy(s_ref, s_out.at[core, me], local_sem.at[1])
-    own = links.send(s_ref, s_out.at[core, me], links.mate)
-    kept_b.start()
-    kept_s.start()
-    links.spread(
-        b_ref.at[core], s_ref, lambda i: b_out.at[i, core], lambda i: s_out.at[core, i]
-    )
-    own.wait_recv()
-    links.drain()
-    kept_b.wait()
-    kept_s.wait()
-
-
-def gather_pair(b_rows, own_start):
-    rows, wide = b_rows.shape
-    width = own_start.shape[1]
-    n = lax.axis_size("bond")
-    b_full, starts = pl.pallas_call(
-        gather_kernel,
-        out_shape=(
-            jax.ShapeDtypeStruct((n, 2, rows // 2, wide), b_rows.dtype),
-            jax.ShapeDtypeStruct((2, n, rows, width), own_start.dtype),
-        ),
-        in_specs=[pl.BlockSpec(memory_space=pltpu.VMEM)] * 2,
-        out_specs=(pl.BlockSpec(memory_space=pl.ANY),) * 2,
-        scratch_shapes=[
-            pltpu.SemaphoreType.DMA((13,)),
-            pltpu.SemaphoreType.DMA((13,)),
-            pltpu.SemaphoreType.DMA((2,)),
-        ],
-        compiler_params=pltpu.CompilerParams(collective_id=0, has_side_effects=True),
-    )(b_rows.reshape(2, rows // 2, wide), own_start)
-    return b_full.reshape(n * rows, wide), starts.reshape(2, n * rows, width)
-
-
-def reduce_kernel(own_ref, out_ref, inc, acc, one, two, send_sem, recv_sem):
+def add(x, y):
+    return x.astype(jnp.float32) + y.astype(jnp.float32)
+
+
+def pair_kernel(
+    gate_ref, bond_ref, site_ref, start_ref, theta_ref, x_ref, gram_ref,
+    ab, used, b_all, s_all, mixed, image, image_t, own, inc, acc, one, two, send_sem, recv_sem, local_sem,
+):
     links = Links(send_sem, recv_sem)
     links.greet((links.x, links.y, links.mate))
     core, me, near, far, across = links.core, links.me, links.near, links.far, links.across
-    half = own_ref.shape[2] // 2
-    low, high = pl.ds(0, half), pl.ds(half, half)
+    send = links.send
+    height, wide = site_ref.shape
+    width = wide // 2
+    left_site = links.chain - core
+    kept_left, kept_mid, kept_right = bond_ref[left_site], bond_ref[left_site + 1], bond_ref[left_site + 2]
+    half = height // 2
+    mine = pl.ds(pl.multiple_of(core * half, half), half)
+    quarter = half // 2
+
+    held = pltpu.make_async_copy(site_ref, ab.at[core], local_sem.at[0])
+    held_start = pltpu.make_async_copy(start_ref, s_all.at[core, me], local_sem.at[1])
+    held.start()
+    held_start.start()
+    first = send(site_ref.at[pl.ds(0, half)], ab.at[core, pl.ds(0, half)], links.mate)
+    second = send(site_ref.at[pl.ds(half, half)], ab.at[core, pl.ds(half, half)], links.mate)
+
+    def s_piece(i, p):
+        return s_all.at[core, i, pl.ds(p * half, half)]
+
+    def s_own(p):
+        return start_ref.at[pl.ds(p * half, half)]
+
+    def b_piece(i, p):
+        return b_all.at[i, core, pl.ds(p * quarter, quarter)]
+
+    def b_own(p):
+        return ab.at[1, pl.ds(pl.multiple_of(core * half + p * quarter, quarter), quarter)]
+
+    s0x = send(s_own(0), s_piece(me, 0), links.x)
+    s1y = send(s_own(1), s_piece(me, 1), links.y)
+    start_mate = send(start_ref, s_all.at[core, me], links.mate)
+    held.wait()
+    first.wait_recv()
+    b0x = send(b_own(0), b_piece(me, 0), links.x)
+    b1y = send(b_own(1), b_piece(me, 1), links.y)
+    second.wait_recv()
+    b1x = send(b_own(1), b_piece(me, 1), links.x)
+    b0y = send(b_own(0), b_piece(me, 0), links.y)
+
+    line = lax.broadcasted_iota(jnp.int32, (height, CHUNK), 0) + me * height
+    lane = lax.broadcasted_iota(jnp.int32, (height, CHUNK), 1)
+
+    def mask(c, carry):
+        for i in range(2):
+            columns = pl.ds(pl.multiple_of(i * width + c * CHUNK, CHUNK), CHUNK)
+            keep = (line < kept_left) & (lane + c * CHUNK < kept_mid)
+            used[:, columns] = jnp.where(keep, ab[0, :, columns].astype(jnp.float32), 0.0).astype(jnp.bfloat16)
+        return carry
+
+    lax.fori_loop(0, width // CHUNK, mask, 0)
+
+    def mix(load, index, fresh):
+        def step(c, carry):
+            columns = pl.ds(pl.multiple_of(c * CHUNK, CHUNK), CHUNK)
+            right = load(columns)
+            for i in range(2):
+                left = used[:, pl.ds(pl.multiple_of(i * width + index * height, height), height)]
+                product = jnp.dot(left, right, preferred_element_type=jnp.float32)
+                mixed[i, :, columns] = product if fresh else mixed[i, :, columns] + product
+            return carry
+
+        lax.fori_loop(0, wide // CHUNK, step, 0)
+
+    def gathered(i):
+        return lambda columns: b_all[i, :, :, columns].reshape(height, CHUNK)
+
+    mix(lambda columns: ab[1, :, columns], me, True)
+
+    s0x.wait_recv()
+    sf_y = send(s_piece(near, 0), s_piece(near, 0), links.y)
+    relay = [send(s_piece(near, 0), s_piece(near, 0), links.mate)]
+    s1y.wait_recv()
+    sf_x = send(s_piece(far, 1), s_piece(far, 1), links.x)
+    relay.append(send(s_piece(far, 1), s_piece(far, 1), links.mate))
+    b0x.wait_recv()
+    bf_y = send(b_piece(near, 0), b_piece(near, 0), links.y)
+    relay_b = [send(b_piece(near, 0), b_piece(near, 0), links.mate)]
+    b1y.wait_recv()
+    bf_x = send(b_piece(far, 1), b_piece(far, 1), links.x)
+    relay_b.append(send(b_piece(far, 1), b_piece(far, 1), links.mate))
+    s1x = send(s_own(1), s_piece(me, 1), links.x)
+    s0y = send(s_own(0), s_piece(me, 0), links.y)
+    b1x.wait_recv()
+    relay_b.append(send(b_piece(near, 1), b_piece(near, 1), links.mate))
+    b0y.wait_recv()
+    relay_b.append(send(b_piece(far, 0), b_piece(far, 0), links.mate))
+    for copy in relay_b:
+        copy.wait_recv()
+    mix(gathered(near), near, False)
+    mix(gathered(far), far, False)
+    sf_y.wait_recv()
+    relay.append(send(s_piece(across, 0), s_piece(across, 0), links.mate))
+    sf_x.wait_recv()
+    relay.append(send(s_piece(across, 1), s_piece(across, 1), links.mate))
+    bf_y.wait_recv()
+    last_b = [send(b_piece(across, 0), b_piece(across, 0), links.mate)]
+    bf_x.wait_recv()
+    last_b.append(send(b_piece(across, 1), b_piece(across, 1), links.mate))
+    for copy in last_b:
+        copy.wait_recv()
+    mix(gathered(across), across, False)
+
+    def form(c, carry):
+        offset = c * CHUNK
+        inside = lane + offset < kept_right
+        parts = []
+        for i in range(2):
+            for j in range(2):
+                columns = pl.ds(pl.multiple_of(j * width + offset, CHUNK), CHUNK)
+                parts.append(jnp.where(inside, mixed[i, :, columns], 0.0))
+        for o in range(2):
+            for q in range(2):
+                row = 4 * (2 * o + q)
+                value = (
+                    gate_ref[left_site, row] * parts[0]
+                    + gate_ref[left_site, row + 1] * parts[1]
+                    + gate_ref[left_site, row + 2] * parts[2]
+                    + gate_ref[left_site, row + 3] * parts[3]
+                )
+                columns = pl.ds(pl.multiple_of(q * width + offset, CHUNK), CHUNK)
+                theta_ref[o, :, columns] = value.astype(jnp.bfloat16)
+        return carry
+
+    lax.fori_loop(0, width // CHUNK, form, 0)
+
+    def apply(q, i, fresh=False):
+        def step(c, carry):
+            columns = pl.ds(pl.multiple_of(c * CHUNK, CHUNK), CHUNK)
+            rows = pl.ds(pl.multiple_of(q * width + i * height, height), height)
+            product = jnp.dot(
+                theta_ref[core, :, rows], s_all[q, i, :, columns], preferred_element_type=jnp.float32
+            )
+            image[:, columns] = product if fresh else image[:, columns] + product
+            return carry
+
+        lax.fori_loop(0, width // CHUNK, step, 0)
+
+    held_start.wait()
+    apply(core, me, True)
+    start_mate.wait_recv()
+    apply(1 - core, me)
+    s1x.wait_recv()
+    relay.append(send(s_piece(near, 1), s_piece(near, 1), links.mate))
+    s0y.wait_recv()
+    relay.append(send(s_piece(far, 0), s_piece(far, 0), links.mate))
+    for i in (across, near, far):
+        apply(core, i)
+    for copy in relay:
+        copy.wait_recv()
+    for i in (across, near, far):
+        apply(1 - core, i)
+
+    def turn(c, carry):
+        columns = pl.ds(pl.multiple_of(c * CHUNK, CHUNK), CHUNK)
+        image_t[columns, :] = jnp.where(lane + c * CHUNK < kept_mid, image[:, columns], 0.0).T.astype(jnp.bfloat16)
+        return carry
+
+    lax.fori_loop(0, width // CHUNK, turn, 0)
+
+    def term(h, i):
+        columns = pl.ds(pl.multiple_of(h * width + i * height, height), height)
+
+        def step(c, carry):
+            rows = pl.ds(pl.multiple_of(c * CHUNK, CHUNK), CHUNK)
+            own[h, i, rows, :] = jnp.dot(
+                image_t[rows, :], theta_ref[core, :, columns], preferred_element_type=jnp.float32
+            ).astype(jnp.bfloat16)
+            return carry
+
+        lax.fori_loop(0, width // CHUNK, step, 0)
+
     order = (across, near, far, me)
-    swaps = [links.send(own_ref.at[1 - core, i], inc.at[i], links.mate) for i in order]
+    swaps = []
+    for i in order:
+        term(1 - core, i)
+        swaps.append(send(own.at[1 - core, i], inc.at[i], links.mate))
+    low, high = pl.ds(0, width // 2), pl.ds(width // 2, width // 2)
 
     def merge(position):
         i = order[position]
+        term(core, i)
         swaps[position].wait_recv()
-        acc[i] = (own_ref[core, i].astype(jnp.float32) + inc[i].astype(jnp.float32)).astype(jnp.bfloat16)
+        acc[i] = add(own[core, i], inc[i]).astype(jnp.bfloat16)
 
     merge(0)
-    x1 = links.send(acc.at[across, low], one.at[0, 1], links.x)
-    y1 = links.send(acc.at[across, high], one.at[1, 1], links.y)
+    x1 = send(acc.at[across, low], one.at[0, 1], links.x)
+    y1 = send(acc.at[across, high], one.at[1, 1], links.y)
     merge(1)
-    x0 = links.send(acc.at[near, low], one.at[0, 0], links.x)
+    x0 = send(acc.at[near, low], one.at[0, 0], links.x)
     merge(2)
-    y0 = links.send(acc.at[far, high], one.at[1, 0], links.y)
+    y0 = send(acc.at[far, high], one.at[1, 0], links.y)
     merge(3)
     x1.wait_recv()
-    two[2] = (acc[far, low].astype(jnp.float32) + one[0, 1].astype(jnp.float32)).astype(jnp.bfloat16)
-    y2 = links.send(two.at[2], two.at[0], links.y)
+    two[2] = add(acc[far, low], one[0, 1]).astype(jnp.bfloat16)
+    y2 = send(two.at[2], two.at[0], links.y)
     y1.wait_recv()
-    two[3] = (acc[near, high].astype(jnp.float32) + one[1, 1].astype(jnp.float32)).astype(jnp.bfloat16)
-    x2 = links.send(two.at[3], two.at[1], links.x)
+    two[3] = add(acc[near, high], one[1, 1]).astype(jnp.bfloat16)
+    x2 = send(two.at[3], two.at[1], links.x)
     x0.wait_recv()
     y2.wait_recv()
-    out_ref[core, me, low] = (
-        acc[me, low].astype(jnp.float32) + one[0, 0].astype(jnp.float32) + two[0].astype(jnp.float32)
-    ).astype(jnp.bfloat16)
+    x_ref[core, me, low] = (add(acc[me, low], one[0, 0]) + two[0].astype(jnp.float32)).astype(jnp.bfloat16)
+
+    def first_of(i):
+        return x_ref.at[core, i, low]
+
+    def second_of(i):
+        return x_ref.at[core, i, high]
+
+    f0 = send(first_of(me), first_of(me), links.y)
+    f1 = send(first_of(me), first_of(me), links.x)
     y0.wait_recv()
     x2.wait_recv()
-    out_ref[core, me, high] = (
-        acc[me, high].astype(jnp.float32) + one[1, 0].astype(jnp.float32) + two[1].astype(jnp.float32)
-    ).astype(jnp.bfloat16)
-    own = links.send(out_ref.at[core, me], out_ref.at[core, me], links.mate)
-    links.spread(
-        out_ref.at[core, me, low],
-        out_ref.at[core, me, high],
-        lambda i: out_ref.at[core, i, low],
-        lambda i: out_ref.at[core, i, high],
-    )
-    own.wait_recv()
+    x_ref[core, me, high] = (add(acc[me, high], one[1, 0]) + two[1].astype(jnp.float32)).astype(jnp.bfloat16)
+    s0 = send(second_of(me), second_of(me), links.x)
+    s1 = send(second_of(me), second_of(me), links.y)
+    whole_mate = send(x_ref.at[core, me], x_ref.at[core, me], links.mate)
+
+    def square(h, i, fresh=False):
+        for k in range(width // CHUNK):
+            rows = slice(k * CHUNK, (k + 1) * CHUNK)
+            product = lax.dot_general(
+                x_ref[h, i, rows, :],
+                x_ref[h, i, k * CHUNK :, :],
+                (((1,), (1,)), ((), ())),
+                preferred_element_type=jnp.float32,
+            )
+            gram_ref[rows, k * CHUNK :] = product if fresh else gram_ref[rows, k * CHUNK :] + product
+
+    square(core, me, True)
+    f0.wait_recv()
+    f2 = send(first_of(far), first_of(far), links.x)
+    late_far = [send(first_of(far), first_of(far), links.mate)]
+    s0.wait_recv()
+    s2 = send(second_of(near), second_of(near), links.y)
+    late_near = [send(second_of(near), second_of(near), links.mate)]
+    f1.wait_recv()
+    late_near.append(send(first_of(near), first_of(near), links.mate))
+    s1.wait_recv()
+    late_far.append(send(second_of(far), second_of(far), links.mate))
+    whole_mate.wait_recv()
+    square(1 - core, me)
+    square(core, near)
+    square(core, far)
+    for copy in late_near:
+        copy.wait_recv()
+    square(1 - core, near)
+    for copy in late_far:
+        copy.wait_recv()
+    square(1 - core, far)
+    f2.wait_recv()
+    late = [send(first_of(across), first_of(across), links.mate)]
+    s2.wait_recv()
+    late.append(send(second_of(across), second_of(across), links.mate))
+    square(core, across)
+    for copy in late:
+        copy.wait_recv()
+    square(1 - core, across)
     links.drain()
 
 
-def reduce_pair(own):
-    total, width = own.shape
+def pair_step(gates, bonds, own_site, own_start):
+    rows, wide = own_site.shape
+    width = wide // 2
     n = lax.axis_size("bond")
-    rows = total // (2 * n)
-    whole = pl.pallas_call(
-        reduce_kernel,
-        out_shape=jax.ShapeDtypeStruct((2, n, rows, width), own.dtype),
-        in_specs=[pl.BlockSpec(memory_space=pltpu.VMEM)],
-        out_specs=pl.BlockSpec(memory_space=pltpu.VMEM),
+    kind = jnp.bfloat16
+    copies = 50
+    return pl.pallas_call(
+        pair_kernel,
+        out_shape=(
+            jax.ShapeDtypeStruct((2, rows, wide), kind),
+            jax.ShapeDtypeStruct((2, n, width, rows), kind),
+            jax.ShapeDtypeStruct((width, width), jnp.float32),
+        ),
+        in_specs=[pl.BlockSpec(memory_space=pltpu.SMEM)] * 2 + [pl.BlockSpec(memory_space=pltpu.VMEM)] * 2,
+        out_specs=(pl.BlockSpec(memory_space=pltpu.VMEM),) * 3,
         scratch_shapes=[
-            pltpu.VMEM((n, rows, width), own.dtype),
-            pltpu.VMEM((n, rows, width), own.dtype),
-            pltpu.VMEM((2, 2, rows // 2, width), own.dtype),
-            pltpu.VMEM((4, rows // 2, width), own.dtype),
-            pltpu.SemaphoreType.DMA((23,)),
-            pltpu.SemaphoreType.DMA((23,)),
+            pltpu.VMEM((2, rows, wide), kind),
+            pltpu.VMEM((rows, wide), kind),
+            pltpu.VMEM((n, 2, rows // 2, wide), kind),
+            pltpu.VMEM((2, n, rows, width), kind),
+            pltpu.VMEM((2, rows, wide), jnp.float32),
+            pltpu.VMEM((rows, width), jnp.float32),
+            pltpu.VMEM((width, rows), kind),
+            pltpu.VMEM((2, n, width, rows), kind),
+            pltpu.VMEM((n, width, rows), kind),
+            pltpu.VMEM((n, width, rows), kind),
+            pltpu.VMEM((2, 2, width // 2, rows), kind),
+            pltpu.VMEM((4, width // 2, rows), kind),
+            pltpu.SemaphoreType.DMA((copies,)),
+            pltpu.SemaphoreType.DMA((copies,)),
+            pltpu.SemaphoreType.DMA((2,)),
         ],
-        compiler_params=pltpu.CompilerParams(collective_id=1, has_side_effects=True),
-    )(own.reshape(2, n, rows, width))
-    return whole.reshape(total, width)
+        compiler_params=pltpu.CompilerParams(
+            collective_id=0, has_side_effects=True, vmem_limit_bytes=56 * 1024 * 1024
+        ),
+    )(gates, bonds, own_site, own_start)
+
+
+def final_kernel(theta_ref, x_ref, inverse_ref, out_ref, square_ref, reduced_ref):
+    core, me = lax.axis_index("chain") % 2, lax.axis_index("bond")
+    n, width, rows = x_ref.shape[1:]
+    nt = (((1,), (1,)), ((), ()))
+
+    @pl.when(core == 0)
+    def _():
+        total = jnp.zeros((SUB, BLOCK), jnp.float32)
+        for o in range(2):
+            def reduce(c, carry):
+                columns = pl.ds(pl.multiple_of(c * CHUNK, CHUNK), CHUNK)
+                value = jnp.zeros((rows, CHUNK), jnp.float32)
+                for h in range(2):
+                    for i in range(n):
+                        at = h * width + i * rows
+                        value = value + lax.dot_general(
+                            theta_ref[o, :, at : at + rows], x_ref[h, i, columns, :], nt,
+                            preferred_element_type=jnp.float32,
+                        )
+                high, low = halves(value)
+                reduced_ref[0, :, columns] = high
+                reduced_ref[1, :, columns] = low
+                return carry
+
+            lax.fori_loop(0, width // CHUNK, reduce, 0)
+            for c in range(width // CHUNK):
+                reach = (c + 1) * CHUNK
+                high, low = halves(inverse_ref[c * CHUNK : reach, :reach])
+                left_high, left_low = reduced_ref[0, :, :reach], reduced_ref[1, :, :reach]
+                value = lax.dot_general(
+                    jnp.concatenate([left_high, left_high, left_low], axis=1),
+                    jnp.concatenate([high, low, high], axis=1),
+                    nt,
+                    preferred_element_type=jnp.float32,
+                )
+                out_ref[:, o * width + c * CHUNK : o * width + reach] = value
+                squared = value * value
+                for j in range(CHUNK // BLOCK):
+                    part = squared[:, j * BLOCK : (j + 1) * BLOCK]
+                    total = total + jnp.sum(part.reshape(rows // SUB, SUB, BLOCK), axis=0)
+        summed = jnp.sum(jnp.sum(total, axis=0, keepdims=True), axis=1, keepdims=True)
+        square_ref[...] = jnp.broadcast_to(summed, (SUB, BLOCK))
+
+    @pl.when(core == 1)
+    def _():
+        high, low = halves(inverse_ref[pl.ds(pl.multiple_of(me * rows, rows), rows), :])
+        for h in range(2):
+            for i in range(n):
+                block = x_ref[h, i]
+                at = h * width + i * rows
+                out_ref[:, at : at + rows] = jnp.dot(
+                    high, block, preferred_element_type=jnp.float32
+                ) + jnp.dot(low, block, preferred_element_type=jnp.float32)
+        square_ref[...] = jnp.zeros((SUB, BLOCK), jnp.float32)
+
+
+def final_rows(thetas, x, inverse):
+    rows, wide = thetas.shape[1:]
+    return pl.pallas_call(
+        final_kernel,
+        out_shape=(
+            jax.ShapeDtypeStruct((rows, wide), jnp.float32),
+            jax.ShapeDtypeStruct((SUB, BLOCK), jnp.float32),
+        ),
+        in_specs=[pl.BlockSpec(memory_space=pltpu.VMEM)] * 3,
+        out_specs=(pl.BlockSpec(memory_space=pltpu.VMEM),) * 2,
+        scratch_shapes=[pltpu.VMEM((2, rows, wide // 2), jnp.bfloat16)],
+        compiler_params=pltpu.CompilerParams(vmem_limit_bytes=56 * 1024 * 1024),
+    )(thetas, x, inverse)
 
 
 def total_kernel(value_ref, out_ref, held, send_sem, recv_sem):
@@ -456,18 +698,41 @@
             pltpu.SemaphoreType.DMA((3,)),
         ],
         compiler_params=pltpu.CompilerParams(collective_id=2, has_side_effects=True),
-    )(jnp.full(shape, value, jnp.float32))[:1, :1]
+    )(value)[:1, :1]
+
+
+def scaled(rows, sum_squares, bond_left, bond_mid, bond_right, is_left):
+    mean_square = (
+        sum_squares / (2.0 * bond_left.astype(jnp.float32) * bond_mid.astype(jnp.float32)) + 1e-06
+    )
+    factor = jnp.where(
+        jnp.full(jnp.shape(mean_square), is_left), lax.rsqrt(mean_square), jnp.sqrt(2.0 * bond_right.astype(jnp.float32))
+    )
+    return (rows * factor)[None]
 
 
 def local(sites, start, gates, bonds):
+    chain_index = lax.axis_index("chain")
+    is_left = chain_index % 2 == 0
+    left_site = jnp.where(is_left, chain_index, chain_index - 1)
+    bond_left = bonds[left_site]
+    bond_mid = bonds[left_site + 1]
+    bond_right = bonds[left_site + 2]
+    bounds = jnp.stack([bond_right, bond_mid, jnp.where(is_left, 0, 1)]).astype(jnp.int32)
+    if lax.axis_size("bond") == 4:
+        thetas, x, gram = pair_step(gates, bonds, sites[0], start[0])
+        inverse = factor_inverse(bounds, gram)
+        rows, squares = final_rows(thetas, x, inverse)
+        return scaled(rows, total_of(squares), bond_left, bond_mid, bond_right, is_left)
+    return spread_out(sites, start, gates, bonds, bounds, is_left, left_site)
+
+
+def spread_out(sites, start, gates, bonds, bounds, is_left, left_site):
     bond_index = lax.axis_index("bond")
-    chain_index = lax.axis_index("chain")
     rank_width = start.shape[2]
     local_rows = sites.shape[1]
     own_site = sites[0]
     own_start = start[0]
-    is_left = chain_index % 2 == 0
-    left_site = jnp.where(is_left, chain_index, chain_index - 1)
     bond_left = bonds[left_site]
     bond_mid = bonds[left_site + 1]
     bond_right = bonds[left_site + 2]
@@ -477,35 +742,30 @@
     other_rows = partner(own_site, "chain", 0)
     a_rows = jnp.where(is_left, own_site, other_rows)
     b_rows = jnp.where(is_left, other_rows, own_site)
-    square = lax.axis_size("bond") == 4
-    if square:
-        b_full, starts = gather_pair(b_rows, own_start)
-    else:
-        b_full = lax.all_gather(b_rows, "bond", axis=0, tiled=True)
-        whole_start = lax.all_gather(own_start, "bond", axis=0, tiled=True)
-        other_start = partner(whole_start, "chain", 0)
-        starts = jnp.stack(
-            [jnp.where(is_left, whole_start, other_start), jnp.where(is_left, other_start, whole_start)]
-        )
+    b_full = lax.all_gather(b_rows, "bond", axis=0, tiled=True)
+    whole_start = lax.all_gather(own_start, "bond", axis=0, tiled=True)
+    other_start = partner(whole_start, "chain", 0)
+    starts = jnp.stack(
+        [jnp.where(is_left, whole_start, other_start), jnp.where(is_left, other_start, whole_start)]
+    )
     left_keep = (row_global < bond_left)[:, None] & jnp.tile(mid_keep, 2)[None, :]
     left_used = jnp.where(left_keep, a_rows, jnp.zeros((), jnp.bfloat16))
-    bounds = jnp.stack([bond_right, bond_mid, jnp.where(is_left, 0, 1)]).astype(jnp.int32)
     thetas, own = theta_terms(gates[left_site], bounds, left_used, b_full, starts)
-    if square:
-        projected_all = reduce_pair(own)
-    else:
-        kept_half = jnp.where(is_left, 0, 1)
-        half_rows = own.shape[0] // 2
-        kept = lax.dynamic_slice_in_dim(own, kept_half * half_rows, half_rows, 0)
-        given = lax.dynamic_slice_in_dim(own, (1 - kept_half) * half_rows, half_rows, 0)
-        both = (kept.astype(jnp.float32) + partner(given, "chain", 0).astype(jnp.float32)).astype(jnp.bfloat16)
-        summed = lax.psum_scatter(both, "bond", scatter_dimension=0, tiled=True)
-        own_half = lax.all_gather(summed, "bond", axis=0, tiled=True)
-        other_half = partner(own_half, "chain", 0)
-        projected_all = jnp.concatenate(
-            [jnp.where(is_left, own_half, other_half), jnp.where(is_left, other_half, own_half)], axis=0
-        )
-    inverse = factor_inverse(bounds, projected_all)
+    kept_half = jnp.where(is_left, 0, 1)
+    half_rows = own.shape[0] // 2
+    kept = lax.dynamic_slice_in_dim(own, kept_half * half_rows, half_rows, 0)
+    given = lax.dynamic_slice_in_dim(own, (1 - kept_half) * half_rows, half_rows, 0)
+    both = (kept.astype(jnp.float32) + partner(given, "chain", 0).astype(jnp.float32)).astype(jnp.bfloat16)
+    summed = lax.psum_scatter(both, "bond", scatter_dimension=0, tiled=True)
+    own_half = lax.all_gather(summed, "bond", axis=0, tiled=True)
+    other_half = partner(own_half, "chain", 0)
+    projected_all = jnp.concatenate(
+        [jnp.where(is_left, own_half, other_half), jnp.where(is_left, other_half, own_half)], axis=0
+    )
+    gram = lax.dot_general(
+        projected_all, projected_all, (((0,), (0,)), ((), ())), preferred_element_type=jnp.float32
+    )
+    inverse = factor_inverse(bounds, gram)
 
     def left_rows():
         reduced = jnp.dot(
@@ -533,14 +793,7 @@
         return basis_rows, jnp.float32(0.0)
 
     rows, squares = lax.cond(is_left, left_rows, right_rows)
-    sum_squares = total_of(squares) if square else lax.psum(squares, "bond")
-    mean_square = (
-        sum_squares / (2.0 * bond_left.astype(jnp.float32) * bond_mid.astype(jnp.float32)) + 1e-06
-    )
-    factor = jnp.where(
-        jnp.full(jnp.shape(mean_square), is_left), lax.rsqrt(mean_square), jnp.sqrt(2.0 * bond_right.astype(jnp.float32))
-    )
-    return (rows * factor)[None]
+    return scaled(rows, lax.psum(squares, "bond"), bond_left, bond_mid, bond_right, is_left)
 
 
 def solution(mesh):

time: 174 us -> 159 us (0.914)
  matrix products: 9.01 us -> 0 us
  other arithmetic: 9.2 us -> 5.03 us
    dot_general x2 -> x0, matrix products: 9.01 us -> none  [the longest x1 5.29 us: left_rows(): jnp.dot(thetas.reshape(2 * local_rows, -1), projected_all, preferred_elem...]
    pallas_call x3 -> x2, Pallas kernels: 104 us -> 107 us  [the longest x1 95.6 us: pair_step(): pl.pallas_call(pair_kernel, out_shape=(jax.ShapeDtypeStruct((2, rows, wid...]
    select_n x1 -> x0, other arithmetic: 3.34 us -> none  [local(): b_rows = jnp.where(is_left, other_rows, own_site)]
    pallas_call x1, Pallas kernels: 37.5 us -> 34.9 us  [factor_inverse(): pl.pallas_call(factor_kernel, out_shape=jax.ShapeDtypeStruct((size, size)...]
  transfers between devices with their start and end apart: 1 -> 0, of which waited for: 0 -> 0; matrix products, arithmetic and copies ran while one was open for 3% -> 0% of each run, Pallas kernels for 0% -> 0%
where the time goes in v2:
time: 159 us; the launch traced here: 158 us
  Pallas kernels  148 us (93%)
  other arithmetic  5.03 us (3%)
  local copies, waits for them, and re-layouts  2.64 us (2%)
  between operations  2.59 us (2%)
    pallas_call x1, Pallas kernels, pair_step(): pl.pallas_call(pair_kernel, out_shape=(jax.ShapeDtypeStruct((2, rows, wid...  95.6 us
    pallas_call x1, Pallas kernels, factor_inverse(): pl.pallas_call(factor_kernel, out_shape=jax.ShapeDtypeStruct((size, size)...  34.9 us
    pallas_call x1, Pallas kernels, final_rows(): pl.pallas_call(final_kernel, out_shape=(jax.ShapeDtypeStruct((rows, wide)...  11.8 us
    pallas_call x1, Pallas kernels, total_of(): pl.pallas_call(total_kernel, out_shape=jax.ShapeDtypeStruct(shape, jnp.fl...  5.9 us

profile of v2, /device:TPU:0, one launch (start us, length us, event | category | flops | bytes accessed | tf_op | source)
XLA Modules:
  0.0 158.4 jit_solution(6222754221049525250)
XLA Ops:
  0.0 1.4 fusion
  3.3 1.9 %pad_add_fusion.bounds_ref = s32[3]{0:T(128)} fusion(s32[1]{0:T(128)} %bitcast.2, s32[1]{0:T(128)} %get-tuple-element.17, s32[1]{0:T(128)} %get-tuple-element.16), kind=kLoop, calls=%fused_computation.1 | loop fusion | flops 6 | bytes 24 | tf_op jit(solution)/shard_map/stack | solution.py:721
  5.2 95.6 %shard_map.46 = (bf16[2,256,2048]{2,1,0:T(8,128)(2,1)}, bf16[2,4,1024,256]{3,2,1,0:T(8,128)(2,1)}, f32[1024,1024]{1,0:T(8,128)}) custom-call(f32[8,16]{1,0:T(8,128)} %gate_ref.1, s32[9]{0:T(128)} %bond_ref.1, bf16[256,2048]{1,0:T(8,128)(2,1)} %bitcast.9, bf16[256,1024]{1,0:T(8,128)(2,1)} %bitcast.10), custom_call_target="tpu_custom_call" | custom-call | tf_op jit(solution)/shard_map/pallas_call | solution.py:574
  100.8 34.9 %shard_map.47.inverse_ref = f32[1024,1024]{1,0:T(8,128)} custom-call(s32[3]{0:T(128)} %pad_add_fusion.bounds_ref, f32[1024,1024]{1,0:T(8,128)} %get-tuple-element.12.gram_ref), custom_call_target="tpu_custom_call" | custom-call | tf_op jit(solution)/shard_map/pallas_call | solution.py:175
  135.7 11.8 %shard_map.48 = (f32[256,2048]{1,0:T(8,128)}, f32[8,128]{1,0:T(8,128)}) custom-call(bf16[2,256,2048]{2,1,0:T(8,128)(2,1)} %get-tuple-element.10.theta_ref, bf16[2,4,1024,256]{3,2,1,0:T(8,128)(2,1)} %get-tuple-element.11.x_ref, f32[1024,1024]{1,0:T(8,128)} %shard_map.47.inverse_ref), custom_call_target="tpu_custom_call" | custom-call | tf_op jit(solution)/shard_map/pallas_call | solution.py:664
  147.5 5.9 %shard_map.49 = f32[8,128]{1,0:T(8,128)} custom-call(f32[8,128]{1,0:T(8,128)} %get-tuple-element.14.value_ref), custom_call_target="tpu_custom_call" | custom-call | tf_op jit(solution)/shard_map/pallas_call | solution.py:690
  153.4 1.2 slice.3
  155.2 3.1 %multiply_bitcast_fusion = f32[1,256,2048]{2,1,0:T(8,128)} fusion(f32[256,2048]{1,0:T(8,128)} %get-tuple-element.13, f32[]{:T(128)} %bitcast.6), kind=kLoop, calls=%fused_computation | loop fusion | flops 524288 | bytes 4194308 | tf_op jit(solution)/shard_map/broadcast_in_dim | solution.py:711

commit v3 on v2

--- a/solution.py
+++ b/solution.py
@@ -275,7 +275,7 @@
             pl.semaphore_signal(barrier, inc=1, device_id=other, device_id_type=MESH)
         pl.semaphore_wait(barrier, len(others))
 
-    def send(self, source, target, device):
+    def plan(self, source, target, device):
         slot = len(self.copies)
         copy = pltpu.make_async_remote_copy(
             src_ref=source,
@@ -285,8 +285,12 @@
             device_id=device,
             device_id_type=MESH,
         )
+        self.copies.append(copy)
+        return copy
+
+    def send(self, source, target, device):
+        copy = self.plan(source, target, device)
         copy.start()
-        self.copies.append(copy)
         return copy
 
     def drain(self):
@@ -299,11 +303,13 @@
 
 
 def pair_kernel(
-    gate_ref, bond_ref, site_ref, start_ref, theta_ref, x_ref, gram_ref,
-    ab, used, b_all, s_all, mixed, image, image_t, own, inc, acc, one, two, send_sem, recv_sem, local_sem,
+    gate_ref, bond_ref, site_ref, start_ref, out_ref, factor_ref,
+    ab, used, b_all, s_all, mixed, image, image_t, own, inc, acc, one, two, theta_ref, x_ref,
+    grams, solved, turned_ref, schur, tile_ref, inverses, sides, product_ref, below, whole, reduced, scalars,
+    send_sem, recv_sem, local_sem,
 ):
     links = Links(send_sem, recv_sem)
-    links.greet((links.x, links.y, links.mate))
+    links.greet((links.x, links.y, links.d, links.mate))
     core, me, near, far, across = links.core, links.me, links.near, links.far, links.across
     send = links.send
     height, wide = site_ref.shape
@@ -311,21 +317,64 @@
     left_site = links.chain - core
     kept_left, kept_mid, kept_right = bond_ref[left_site], bond_ref[left_site + 1], bond_ref[left_site + 2]
     half = height // 2
-    mine = pl.ds(pl.multiple_of(core * half, half), half)
     quarter = half // 2
 
+    parts = 2
+    span = width // parts
     held = pltpu.make_async_copy(site_ref, ab.at[core], local_sem.at[0])
-    held_start = pltpu.make_async_copy(start_ref, s_all.at[core, me], local_sem.at[1])
     held.start()
-    held_start.start()
     first = send(site_ref.at[pl.ds(0, half)], ab.at[core, pl.ds(0, half)], links.mate)
     second = send(site_ref.at[pl.ds(half, half)], ab.at[core, pl.ds(half, half)], links.mate)
 
-    def s_piece(i, p):
-        return s_all.at[core, i, pl.ds(p * half, half)]
-
-    def s_own(p):
-        return start_ref.at[pl.ds(p * half, half)]
+    def s_block(k, i):
+        return s_all.at[k, core, i]
+
+    def s_piece(k, i, p):
+        return s_all.at[k, core, i, pl.ds(p * half, half)]
+
+    def s_own(k, p):
+        return start_ref.at[pl.ds(p * half, half), pl.ds(k * span, span)]
+
+    starts = []
+    for k in range(parts):
+        whole_own = start_ref.at[:, pl.ds(k * span, span)]
+        starts.append(
+            dict(
+                held=pltpu.make_async_copy(whole_own, s_block(k, me), local_sem.at[1 + k]),
+                mate=links.plan(whole_own, s_block(k, me), links.mate),
+                x0=links.plan(s_own(k, 0), s_piece(k, me, 0), links.x),
+                y1=links.plan(s_own(k, 1), s_piece(k, me, 1), links.y),
+                x1=links.plan(s_own(k, 1), s_piece(k, me, 1), links.x),
+                y0=links.plan(s_own(k, 0), s_piece(k, me, 0), links.y),
+                forward_y=links.plan(s_piece(k, near, 0), s_piece(k, near, 0), links.y),
+                forward_x=links.plan(s_piece(k, far, 1), s_piece(k, far, 1), links.x),
+                mate_near=links.plan(s_block(k, near), s_block(k, near), links.mate),
+                mate_far=links.plan(s_block(k, far), s_block(k, far), links.mate),
+                mate_across=links.plan(s_block(k, across), s_block(k, across), links.mate),
+            )
+        )
+
+    def s_go(k, *names):
+        for name in names:
+            starts[k][name].start()
+
+    def s_wait(k, *names):
+        for name in names:
+            starts[k][name].wait_recv()
+
+    def s_forward(k):
+        s_wait(k, "x0")
+        s_go(k, "forward_y")
+        s_wait(k, "y1")
+        s_go(k, "forward_x")
+
+    def s_to_mate(k):
+        s_wait(k, "x1")
+        s_go(k, "mate_near")
+        s_wait(k, "y0")
+        s_go(k, "mate_far")
+        s_wait(k, "forward_y", "forward_x")
+        s_go(k, "mate_across")
 
     def b_piece(i, p):
         return b_all.at[i, core, pl.ds(p * quarter, quarter)]
@@ -333,9 +382,7 @@
     def b_own(p):
         return ab.at[1, pl.ds(pl.multiple_of(core * half + p * quarter, quarter), quarter)]
 
-    s0x = send(s_own(0), s_piece(me, 0), links.x)
-    s1y = send(s_own(1), s_piece(me, 1), links.y)
-    start_mate = send(start_ref, s_all.at[core, me], links.mate)
+    s_go(0, "x0", "y1", "mate", "held")
     held.wait()
     first.wait_recv()
     b0x = send(b_own(0), b_piece(me, 0), links.x)
@@ -355,6 +402,7 @@
         return carry
 
     lax.fori_loop(0, width // CHUNK, mask, 0)
+    whole[...] = jnp.zeros_like(whole)
 
     def mix(load, index, fresh):
         def step(c, carry):
@@ -373,32 +421,23 @@
 
     mix(lambda columns: ab[1, :, columns], me, True)
 
-    s0x.wait_recv()
-    sf_y = send(s_piece(near, 0), s_piece(near, 0), links.y)
-    relay = [send(s_piece(near, 0), s_piece(near, 0), links.mate)]
-    s1y.wait_recv()
-    sf_x = send(s_piece(far, 1), s_piece(far, 1), links.x)
-    relay.append(send(s_piece(far, 1), s_piece(far, 1), links.mate))
+    s_forward(0)
     b0x.wait_recv()
     bf_y = send(b_piece(near, 0), b_piece(near, 0), links.y)
     relay_b = [send(b_piece(near, 0), b_piece(near, 0), links.mate)]
     b1y.wait_recv()
     bf_x = send(b_piece(far, 1), b_piece(far, 1), links.x)
     relay_b.append(send(b_piece(far, 1), b_piece(far, 1), links.mate))
-    s1x = send(s_own(1), s_piece(me, 1), links.x)
-    s0y = send(s_own(0), s_piece(me, 0), links.y)
+    s_go(0, "x1", "y0")
     b1x.wait_recv()
     relay_b.append(send(b_piece(near, 1), b_piece(near, 1), links.mate))
     b0y.wait_recv()
     relay_b.append(send(b_piece(far, 0), b_piece(far, 0), links.mate))
+    s_go(1, "x0", "y1", "mate", "held")
     for copy in relay_b:
         copy.wait_recv()
     mix(gathered(near), near, False)
     mix(gathered(far), far, False)
-    sf_y.wait_recv()
-    relay.append(send(s_piece(across, 0), s_piece(across, 0), links.mate))
-    sf_x.wait_recv()
-    relay.append(send(s_piece(across, 1), s_piece(across, 1), links.mate))
     bf_y.wait_recv()
     last_b = [send(b_piece(across, 0), b_piece(across, 0), links.mate)]
     bf_x.wait_recv()
@@ -430,138 +469,335 @@
 
     lax.fori_loop(0, width // CHUNK, form, 0)
 
-    def apply(q, i, fresh=False):
+    def apply(k, q, i, fresh=False):
         def step(c, carry):
             columns = pl.ds(pl.multiple_of(c * CHUNK, CHUNK), CHUNK)
+            there = pl.ds(pl.multiple_of(k * span + c * CHUNK, CHUNK), CHUNK)
             rows = pl.ds(pl.multiple_of(q * width + i * height, height), height)
             product = jnp.dot(
-                theta_ref[core, :, rows], s_all[q, i, :, columns], preferred_element_type=jnp.float32
+                theta_ref[core, :, rows], s_all[k, q, i, :, columns], preferred_element_type=jnp.float32
             )
-            image[:, columns] = product if fresh else image[:, columns] + product
+            image[:, there] = product if fresh else image[:, there] + product
             return carry
 
-        lax.fori_loop(0, width // CHUNK, step, 0)
-
-    held_start.wait()
-    apply(core, me, True)
-    start_mate.wait_recv()
-    apply(1 - core, me)
-    s1x.wait_recv()
-    relay.append(send(s_piece(near, 1), s_piece(near, 1), links.mate))
-    s0y.wait_recv()
-    relay.append(send(s_piece(far, 0), s_piece(far, 0), links.mate))
-    for i in (across, near, far):
-        apply(core, i)
-    for copy in relay:
-        copy.wait_recv()
-    for i in (across, near, far):
-        apply(1 - core, i)
-
-    def turn(c, carry):
-        columns = pl.ds(pl.multiple_of(c * CHUNK, CHUNK), CHUNK)
-        image_t[columns, :] = jnp.where(lane + c * CHUNK < kept_mid, image[:, columns], 0.0).T.astype(jnp.bfloat16)
-        return carry
-
-    lax.fori_loop(0, width // CHUNK, turn, 0)
-
-    def term(h, i):
+        lax.fori_loop(0, span // CHUNK, step, 0)
+
+    def imaged(k):
+        starts[k]["held"].wait()
+        apply(k, core, me, True)
+        for i in (near, far, across):
+            apply(k, core, i)
+        s_wait(k, "mate")
+        apply(k, 1 - core, me)
+        for i, name in ((near, "mate_near"), (far, "mate_far"), (across, "mate_across")):
+            s_wait(k, name)
+            apply(k, 1 - core, i)
+
+        def turn(c, carry):
+            columns = pl.ds(pl.multiple_of(k * span + c * CHUNK, CHUNK), CHUNK)
+            kept = lane + k * span + c * CHUNK < kept_mid
+            image_t[columns, :] = jnp.where(kept, image[:, columns], 0.0).T.astype(jnp.bfloat16)
+            return carry
+
+        lax.fori_loop(0, span // CHUNK, turn, 0)
+
+    def term(k, h, i):
         columns = pl.ds(pl.multiple_of(h * width + i * height, height), height)
 
         def step(c, carry):
-            rows = pl.ds(pl.multiple_of(c * CHUNK, CHUNK), CHUNK)
+            rows = pl.ds(pl.multiple_of(k * span + c * CHUNK, CHUNK), CHUNK)
             own[h, i, rows, :] = jnp.dot(
                 image_t[rows, :], theta_ref[core, :, columns], preferred_element_type=jnp.float32
             ).astype(jnp.bfloat16)
             return carry
 
-        lax.fori_loop(0, width // CHUNK, step, 0)
+        lax.fori_loop(0, span // CHUNK, step, 0)
 
     order = (across, near, far, me)
-    swaps = []
-    for i in order:
-        term(1 - core, i)
-        swaps.append(send(own.at[1 - core, i], inc.at[i], links.mate))
-    low, high = pl.ds(0, width // 2), pl.ds(width // 2, width // 2)
-
-    def merge(position):
-        i = order[position]
-        term(core, i)
-        swaps[position].wait_recv()
-        acc[i] = add(own[core, i], inc[i]).astype(jnp.bfloat16)
-
-    merge(0)
-    x1 = send(acc.at[across, low], one.at[0, 1], links.x)
-    y1 = send(acc.at[across, high], one.at[1, 1], links.y)
-    merge(1)
-    x0 = send(acc.at[near, low], one.at[0, 0], links.x)
-    merge(2)
-    y0 = send(acc.at[far, high], one.at[1, 0], links.y)
-    merge(3)
-    x1.wait_recv()
-    two[2] = add(acc[far, low], one[0, 1]).astype(jnp.bfloat16)
-    y2 = send(two.at[2], two.at[0], links.y)
-    y1.wait_recv()
-    two[3] = add(acc[near, high], one[1, 1]).astype(jnp.bfloat16)
-    x2 = send(two.at[3], two.at[1], links.x)
-    x0.wait_recv()
-    y2.wait_recv()
-    x_ref[core, me, low] = (add(acc[me, low], one[0, 0]) + two[0].astype(jnp.float32)).astype(jnp.bfloat16)
-
-    def first_of(i):
-        return x_ref.at[core, i, low]
-
-    def second_of(i):
-        return x_ref.at[core, i, high]
-
-    f0 = send(first_of(me), first_of(me), links.y)
-    f1 = send(first_of(me), first_of(me), links.x)
-    y0.wait_recv()
-    x2.wait_recv()
-    x_ref[core, me, high] = (add(acc[me, high], one[1, 0]) + two[1].astype(jnp.float32)).astype(jnp.bfloat16)
-    s0 = send(second_of(me), second_of(me), links.x)
-    s1 = send(second_of(me), second_of(me), links.y)
-    whole_mate = send(x_ref.at[core, me], x_ref.at[core, me], links.mate)
-
-    def square(h, i, fresh=False):
-        for k in range(width // CHUNK):
-            rows = slice(k * CHUNK, (k + 1) * CHUNK)
-            product = lax.dot_general(
-                x_ref[h, i, rows, :],
-                x_ref[h, i, k * CHUNK :, :],
-                (((1,), (1,)), ((), ())),
+    sums = [{} for _ in range(parts)]
+
+    def low(k):
+        return pl.ds(k * span, span // 2)
+
+    def high(k):
+        return pl.ds(k * span + span // 2, span // 2)
+
+    def exchange(k):
+        both = pl.ds(k * span, span)
+        sums[k]["swaps"] = []
+        for i in order:
+            term(k, 1 - core, i)
+            sums[k]["swaps"].append(send(own.at[1 - core, i, both], inc.at[i, both], links.mate))
+
+    def reduce_first(k):
+        both = pl.ds(k * span, span)
+
+        def merge(position):
+            i = order[position]
+            term(k, core, i)
+            sums[k]["swaps"][position].wait_recv()
+            acc[i, both] = add(own[core, i, both], inc[i, both]).astype(jnp.bfloat16)
+
+        merge(0)
+        sums[k]["x1"] = send(acc.at[across, low(k)], one.at[k, 0, 1], links.x)
+        sums[k]["y1"] = send(acc.at[across, high(k)], one.at[k, 1, 1], links.y)
+        merge(1)
+        sums[k]["x0"] = send(acc.at[near, low(k)], one.at[k, 0, 0], links.x)
+        merge(2)
+        sums[k]["y0"] = send(acc.at[far, high(k)], one.at[k, 1, 0], links.y)
+        merge(3)
+
+    def reduce_second(k):
+        sums[k]["x1"].wait_recv()
+        two[k, 2] = add(acc[far, low(k)], one[k, 0, 1]).astype(jnp.bfloat16)
+        sums[k]["y2"] = send(two.at[k, 2], two.at[k, 0], links.y)
+        sums[k]["y1"].wait_recv()
+        two[k, 3] = add(acc[near, high(k)], one[k, 1, 1]).astype(jnp.bfloat16)
+        sums[k]["x2"] = send(two.at[k, 3], two.at[k, 1], links.x)
+
+    def reduce_last(k, part):
+        for name, n, where in (("0", 0, low(k)), ("1", 1, high(k))):
+            sums[k][("x0", "y0")[n]].wait_recv()
+            sums[k][("y2", "x2")[n]].wait_recv()
+            value = add(acc[me, where], one[k, n, 0]) + two[k, n].astype(jnp.float32)
+            value = value.astype(jnp.bfloat16)
+            x_ref[core, me, where] = value
+            value = value.astype(jnp.float32)
+            value = jnp.sum((value * value).reshape(span // 2 // SUB, SUB, height), axis=0)
+            for j in range(height // BLOCK):
+                part = part + value[:, j * BLOCK : (j + 1) * BLOCK]
+        return part
+
+    s_to_mate(0)
+    imaged(0)
+    s_forward(1)
+    s_go(1, "x1", "y0")
+    exchange(0)
+    reduce_first(0)
+    s_to_mate(1)
+    reduce_second(0)
+    imaged(1)
+    exchange(1)
+    reduce_first(1)
+    part = reduce_last(0, jnp.zeros((SUB, BLOCK), jnp.float32))
+    reduce_second(1)
+
+    def piece(i, c, p):
+        return x_ref.at[core, i, pl.ds(c * CHUNK + p * BLOCK, BLOCK)]
+
+    def chunk_of(i, c):
+        return x_ref.at[core, i, pl.ds(c * CHUNK, CHUNK)]
+
+    chunks = width // CHUNK
+    plans = []
+    for c in range(chunks):
+        plans.append(
+            dict(
+                y0=links.plan(piece(me, c, 0), piece(me, c, 0), links.y),
+                x1=links.plan(piece(me, c, 1), piece(me, c, 1), links.x),
+                x0=links.plan(piece(me, c, 0), piece(me, c, 0), links.x),
+                y1=links.plan(piece(me, c, 1), piece(me, c, 1), links.y),
+                mate=links.plan(chunk_of(me, c), chunk_of(me, c), links.mate),
+                forward_x=links.plan(piece(far, c, 0), piece(far, c, 0), links.x),
+                forward_y=links.plan(piece(near, c, 1), piece(near, c, 1), links.y),
+                mate_near=links.plan(chunk_of(near, c), chunk_of(near, c), links.mate),
+                mate_far=links.plan(chunk_of(far, c), chunk_of(far, c), links.mate),
+                mate_across=links.plan(chunk_of(across, c), chunk_of(across, c), links.mate),
+            )
+        )
+
+    def offer(c):
+        for name in ("y0", "x1", "x0", "y1", "mate"):
+            plans[c][name].start()
+
+    def pass_on(c):
+        plans[c]["y0"].wait_recv()
+        plans[c]["forward_x"].start()
+        plans[c]["x1"].wait_recv()
+        plans[c]["forward_y"].start()
+
+    def to_mate(c):
+        plans[c]["x0"].wait_recv()
+        plans[c]["mate_near"].start()
+        plans[c]["y1"].wait_recv()
+        plans[c]["mate_far"].start()
+
+    def last_to_mate(c):
+        plans[c]["forward_x"].wait_recv()
+        plans[c]["forward_y"].wait_recv()
+        plans[c]["mate_across"].start()
+
+    def arrive(c):
+        for name in ("mate", "mate_near", "mate_far", "mate_across"):
+            plans[c][name].wait_recv()
+
+    offer(0)
+    part = reduce_last(1, part)
+
+    def spread_sum(value, at, others):
+        scalars[at] = value
+        copies = [send(scalars.at[at], scalars.at[at + 1 + n], other) for n, other in enumerate(others)]
+        for n, copy in enumerate(copies):
+            copy.wait_recv()
+            value = value + scalars[at + 1 + n]
+        return value
+
+    part = spread_sum(part, 0, (links.mate,))
+    pass_on(0)
+    offer(1)
+    part = spread_sum(part, 2, (links.x, links.y, links.d))
+    trace = jnp.sum(jnp.sum(part, axis=0, keepdims=True), axis=1, keepdims=True)
+    ridge = ridge_ratio * trace / jnp.full((1, 1), kept_mid, jnp.int32).astype(jnp.float32)
+    unit, root = 1.0 / ridge, lax.rsqrt(ridge)
+    to_mate(0)
+    last_to_mate(0)
+    arrive(0)
+
+    nt = (((1,), (1,)), ((), ()))
+    blocks = [(h, i) for h in range(2) for i in range(width // height)]
+    eye = lax.broadcasted_iota(jnp.int32, (CHUNK, CHUNK), 0) == lax.broadcasted_iota(jnp.int32, (CHUNK, CHUNK), 1)
+    scalars[6] = jnp.zeros((SUB, BLOCK), jnp.float32)
+    inverses[...] = jnp.zeros_like(inverses)
+    sides[...] = jnp.zeros_like(sides)
+
+    def upper(c, o, lines):
+        reach = (c + 1) * CHUNK
+        here = slice(reach - CHUNK, reach)
+        value = lax.dot_general(
+            jnp.concatenate([reduced[0, lines, :reach], reduced[0, lines, :reach], reduced[1, lines, :reach]], axis=1),
+            jnp.concatenate([whole[0, here, :reach], whole[1, here, :reach], whole[0, here, :reach]], axis=1),
+            nt, preferred_element_type=jnp.float32,
+        )
+        out_ref[:, pl.ds(pl.multiple_of(o * width + reach - CHUNK, CHUNK), CHUNK)] = value
+        squared = jnp.sum((value * value).reshape(height // SUB, SUB, CHUNK), axis=0)
+        part = squared[:, :BLOCK]
+        for j in range(1, CHUNK // BLOCK):
+            part = part + squared[:, j * BLOCK : (j + 1) * BLOCK]
+        scalars[6] = scalars[6] + part
+
+    for c in range(chunks):
+        start = c * CHUNK
+        reach = start + CHUNK
+        here = slice(start, reach)
+        for j in range(c + 1):
+            value = jnp.zeros((CHUNK, CHUNK), jnp.float32)
+            for h, i in blocks:
+                value = value + lax.dot_general(
+                    x_ref[h, i, j * CHUNK : (j + 1) * CHUNK, :], x_ref[h, i, here, :], nt,
+                    preferred_element_type=jnp.float32,
+                )
+            grams[j * CHUNK : (j + 1) * CHUNK, :] = value
+        value = grams[here, :]
+        if c > 0:
+            for j in range(c):
+                to = (j + 1) * CHUNK
+                row = slice(j * CHUNK, to)
+                solved[row, :] = jnp.dot(
+                    jnp.concatenate([whole[0, row, :to], whole[0, row, :to], whole[1, row, :to]], axis=1),
+                    threefold(grams[:to, :]),
+                    preferred_element_type=jnp.float32,
+                )
+            turned_ref[:, : 3 * start] = threewide(solved[:start, :].T)
+            value = value - jnp.dot(
+                turned_ref[:, : 3 * start], threefold(solved[:start, :]), preferred_element_type=jnp.float32
+            )
+        schur[...] = value + jnp.where(eye, ridge, 0.0)
+        tile_ref[...] = unit * schur[:BLOCK, :BLOCK]
+
+        def panel(p, carry, c=c, start=start):
+            lines = pl.ds(pl.multiple_of(p * BLOCK, BLOCK), BLOCK)
+            columns = pl.ds(pl.multiple_of(start + p * BLOCK, BLOCK), BLOCK)
+            inverse = diagonal_inverse(tile_ref[...]) * root
+            value = jnp.zeros((2 * height, BLOCK), jnp.float32)
+            for h, i in blocks:
+                at = h * width + i * height
+                value = value + lax.dot_general(
+                    theta_ref[:, :, at : at + height].reshape(2 * height, height), x_ref[h, i, columns, :], nt,
+                    preferred_element_type=jnp.float32,
+                )
+            top, low_part = halves(value)
+            reduced[0, :, columns] = top
+            reduced[1, :, columns] = low_part
+            if c > 0:
+                product_ref[lines, :start] = jnp.dot(
+                    turned_ref[lines, : 3 * start],
+                    jnp.concatenate([whole[0, :start, :start], whole[1, :start, :start], whole[0, :start, :start]], axis=0),
+                    preferred_element_type=jnp.float32,
+                )
+            if c > 0:
+                upper(c - 1, p, pl.ds(pl.multiple_of(p * height, height), height))
+            below[...] = jnp.dot(threewide(sides[...].T), threefold(inverses[0]), preferred_element_type=jnp.float32)
+            inverses[p] = inverse
+
+            @pl.when(p == 0)
+            def _():
+                side = jnp.dot(threewide(inverses[0]), threefold(schur[:BLOCK, BLOCK:]), preferred_element_type=jnp.float32)
+                sides[...] = side
+                tile_ref[...] = unit * (
+                    schur[BLOCK:, BLOCK:]
+                    - jnp.dot(threewide(side.T), threefold(side), preferred_element_type=jnp.float32)
+                )
+                if c + 1 < chunks:
+                    pass_on(c + 1)
+                    to_mate(c + 1)
+                    if c + 2 < chunks:
+                        offer(c + 2)
+
+            if c + 1 < chunks:
+
+                @pl.when(p == 1)
+                def _():
+                    last_to_mate(c + 1)
+
+            return carry
+
+        lax.fori_loop(0, CHUNK // BLOCK, panel, 0)
+        corner = -jnp.dot(threewide(inverses[1]), threefold(below[...]), preferred_element_type=jnp.float32)
+        own_inverse = jnp.concatenate(
+            [
+                jnp.concatenate([inverses[0], jnp.zeros((BLOCK, BLOCK), jnp.float32)], axis=1),
+                jnp.concatenate([corner, inverses[1]], axis=1),
+            ],
+            axis=0,
+        )
+        top, low_part = halves(own_inverse)
+        whole[0, here, here] = top
+        whole[1, here, here] = low_part
+        if c > 0:
+            lead = -jnp.dot(
+                jnp.concatenate([top, top, low_part], axis=1), threefold(product_ref[:, :start]),
                 preferred_element_type=jnp.float32,
             )
-            gram_ref[rows, k * CHUNK :] = product if fresh else gram_ref[rows, k * CHUNK :] + product
-
-    square(core, me, True)
-    f0.wait_recv()
-    f2 = send(first_of(far), first_of(far), links.x)
-    late_far = [send(first_of(far), first_of(far), links.mate)]
-    s0.wait_recv()
-    s2 = send(second_of(near), second_of(near), links.y)
-    late_near = [send(second_of(near), second_of(near), links.mate)]
-    f1.wait_recv()
-    late_near.append(send(first_of(near), first_of(near), links.mate))
-    s1.wait_recv()
-    late_far.append(send(second_of(far), second_of(far), links.mate))
-    whole_mate.wait_recv()
-    square(1 - core, me)
-    square(core, near)
-    square(core, far)
-    for copy in late_near:
-        copy.wait_recv()
-    square(1 - core, near)
-    for copy in late_far:
-        copy.wait_recv()
-    square(1 - core, far)
-    f2.wait_recv()
-    late = [send(first_of(across), first_of(across), links.mate)]
-    s2.wait_recv()
-    late.append(send(second_of(across), second_of(across), links.mate))
-    square(core, across)
-    for copy in late:
-        copy.wait_recv()
-    square(1 - core, across)
+            top, low_part = halves(lead)
+            whole[0, here, :start] = top
+            whole[1, here, :start] = low_part
+
+        if c + 1 < chunks:
+            arrive(c + 1)
+
+    @pl.when(core == 0)
+    def _():
+        for o in range(2):
+            upper(chunks - 1, o, slice(o * height, (o + 1) * height))
+
+    @pl.when(core == 1)
+    def _():
+        rows = pl.ds(pl.multiple_of(me * height, height), height)
+        for h, i in blocks:
+            at = h * width + i * height
+            out_ref[:, at : at + height] = jnp.dot(
+                whole[0, rows, :], x_ref[h, i], preferred_element_type=jnp.float32
+            ) + jnp.dot(whole[1, rows, :], x_ref[h, i], preferred_element_type=jnp.float32)
+
+    total = spread_sum(scalars[6], 7, (links.x, links.y, links.d))
+    total = jnp.sum(jnp.sum(total, axis=0, keepdims=True), axis=1, keepdims=True)
+
+    def real(value):
+        return jnp.full((1, 1), value, jnp.int32).astype(jnp.float32)
+
+    mean_square = total / (2.0 * real(kept_left) * real(kept_mid)) + 1e-06
+    factor = jnp.where(core == 0, lax.rsqrt(mean_square), jnp.sqrt(2.0 * real(kept_right)))
+    factor_ref[...] = jnp.broadcast_to(factor, (SUB, BLOCK))
     links.drain()
 
 
@@ -570,135 +806,50 @@
     width = wide // 2
     n = lax.axis_size("bond")
     kind = jnp.bfloat16
-    copies = 50
+    copies = 112
     return pl.pallas_call(
         pair_kernel,
         out_shape=(
-            jax.ShapeDtypeStruct((2, rows, wide), kind),
-            jax.ShapeDtypeStruct((2, n, width, rows), kind),
-            jax.ShapeDtypeStruct((width, width), jnp.float32),
+            jax.ShapeDtypeStruct((rows, wide), jnp.float32),
+            jax.ShapeDtypeStruct((SUB, BLOCK), jnp.float32),
         ),
-        in_specs=[pl.BlockSpec(memory_space=pltpu.SMEM)] * 2 + [pl.BlockSpec(memory_space=pltpu.VMEM)] * 2,
-        out_specs=(pl.BlockSpec(memory_space=pltpu.VMEM),) * 3,
+        in_specs=[pl.BlockSpec(memory_space=pltpu.SMEM)] * 2 + [pl.BlockSpec(memory_space=pltpu.HBM)] * 2,
+        out_specs=(pl.BlockSpec(memory_space=pltpu.VMEM),) * 2,
         scratch_shapes=[
             pltpu.VMEM((2, rows, wide), kind),
             pltpu.VMEM((rows, wide), kind),
             pltpu.VMEM((n, 2, rows // 2, wide), kind),
-            pltpu.VMEM((2, n, rows, width), kind),
+            pltpu.VMEM((2, 2, n, rows, width // 2), kind),
             pltpu.VMEM((2, rows, wide), jnp.float32),
             pltpu.VMEM((rows, width), jnp.float32),
             pltpu.VMEM((width, rows), kind),
             pltpu.VMEM((2, n, width, rows), kind),
             pltpu.VMEM((n, width, rows), kind),
             pltpu.VMEM((n, width, rows), kind),
-            pltpu.VMEM((2, 2, width // 2, rows), kind),
-            pltpu.VMEM((4, width // 2, rows), kind),
+            pltpu.VMEM((2, 2, 2, width // 4, rows), kind),
+            pltpu.VMEM((2, 4, width // 4, rows), kind),
+            pltpu.VMEM((2, rows, wide), kind),
+            pltpu.VMEM((2, n, width, rows), kind),
+            pltpu.VMEM((width, CHUNK), jnp.float32),
+            pltpu.VMEM((width, CHUNK), jnp.float32),
+            pltpu.VMEM((CHUNK, 3 * width), kind),
+            pltpu.VMEM((CHUNK, CHUNK), jnp.float32),
+            pltpu.VMEM((BLOCK, BLOCK), jnp.float32),
+            pltpu.VMEM((2, BLOCK, BLOCK), jnp.float32),
+            pltpu.VMEM((BLOCK, BLOCK), jnp.float32),
+            pltpu.VMEM((CHUNK, width), jnp.float32),
+            pltpu.VMEM((BLOCK, BLOCK), jnp.float32),
+            pltpu.VMEM((2, width, width), kind),
+            pltpu.VMEM((2, 2 * rows, width), kind),
+            pltpu.VMEM((11, SUB, BLOCK), jnp.float32),
             pltpu.SemaphoreType.DMA((copies,)),
             pltpu.SemaphoreType.DMA((copies,)),
-            pltpu.SemaphoreType.DMA((2,)),
+            pltpu.SemaphoreType.DMA((3,)),
         ],
         compiler_params=pltpu.CompilerParams(
-            collective_id=0, has_side_effects=True, vmem_limit_bytes=56 * 1024 * 1024
+            collective_id=0, has_side_effects=True, vmem_limit_bytes=57 * 1024 * 1024
         ),
     )(gates, bonds, own_site, own_start)
-
-
-def final_kernel(theta_ref, x_ref, inverse_ref, out_ref, square_ref, reduced_ref):
-    core, me = lax.axis_index("chain") % 2, lax.axis_index("bond")
-    n, width, rows = x_ref.shape[1:]
-    nt = (((1,), (1,)), ((), ()))
-
-    @pl.when(core == 0)
-    def _():
-        total = jnp.zeros((SUB, BLOCK), jnp.float32)
-        for o in range(2):
-            def reduce(c, carry):
-                columns = pl.ds(pl.multiple_of(c * CHUNK, CHUNK), CHUNK)
-                value = jnp.zeros((rows, CHUNK), jnp.float32)
-                for h in range(2):
-                    for i in range(n):
-                        at = h * width + i * rows
-                        value = value + lax.dot_general(
-                            theta_ref[o, :, at : at + rows], x_ref[h, i, columns, :], nt,
-                            preferred_element_type=jnp.float32,
-                        )
-                high, low = halves(value)
-                reduced_ref[0, :, columns] = high
-                reduced_ref[1, :, columns] = low
-                return carry
-
-            lax.fori_loop(0, width // CHUNK, reduce, 0)
-            for c in range(width // CHUNK):
-                reach = (c + 1) * CHUNK
-                high, low = halves(inverse_ref[c * CHUNK : reach, :reach])
-                left_high, left_low = reduced_ref[0, :, :reach], reduced_ref[1, :, :reach]
-                value = lax.dot_general(
-                    jnp.concatenate([left_high, left_high, left_low], axis=1),
-                    jnp.concatenate([high, low, high], axis=1),
-                    nt,
-                    preferred_element_type=jnp.float32,
-                )
-                out_ref[:, o * width + c * CHUNK : o * width + reach] = value
-                squared = value * value
-                for j in range(CHUNK // BLOCK):
-                    part = squared[:, j * BLOCK : (j + 1) * BLOCK]
-                    total = total + jnp.sum(part.reshape(rows // SUB, SUB, BLOCK), axis=0)
-        summed = jnp.sum(jnp.sum(total, axis=0, keepdims=True), axis=1, keepdims=True)
-        square_ref[...] = jnp.broadcast_to(summed, (SUB, BLOCK))
-
-    @pl.when(core == 1)
-    def _():
-        high, low = halves(inverse_ref[pl.ds(pl.multiple_of(me * rows, rows), rows), :])
-        for h in range(2):
-            for i in range(n):
-                block = x_ref[h, i]
-                at = h * width + i * rows
-                out_ref[:, at : at + rows] = jnp.dot(
-                    high, block, preferred_element_type=jnp.float32
-                ) + jnp.dot(low, block, preferred_element_type=jnp.float32)
-        square_ref[...] = jnp.zeros((SUB, BLOCK), jnp.float32)
-
-
-def final_rows(thetas, x, inverse):
-    rows, wide = thetas.shape[1:]
-    return pl.pallas_call(
-        final_kernel,
-        out_shape=(
-            jax.ShapeDtypeStruct((rows, wide), jnp.float32),
-            jax.ShapeDtypeStruct((SUB, BLOCK), jnp.float32),
-        ),
-        in_specs=[pl.BlockSpec(memory_space=pltpu.VMEM)] * 3,
-        out_specs=(pl.BlockSpec(memory_space=pltpu.VMEM),) * 2,
-        scratch_shapes=[pltpu.VMEM((2, rows, wide // 2), jnp.bfloat16)],
-        compiler_params=pltpu.CompilerParams(vmem_limit_bytes=56 * 1024 * 1024),
-    )(thetas, x, inverse)
-
-
-def total_kernel(value_ref, out_ref, held, send_sem, recv_sem):
-    links = Links(send_sem, recv_sem)
-    others = (links.x, links.y, links.d)
-    links.greet(others)
-    copies = [links.send(value_ref, held.at[i], other) for i, other in enumerate(others)]
-    for copy in copies:
-        copy.wait_recv()
-    out_ref[...] = (value_ref[...] + held[2]) + (held[0] + held[1])
-    links.drain()
-
-
-def total_of(value):
-    shape = (8, 128)
-    return pl.pallas_call(
-        total_kernel,
-        out_shape=jax.ShapeDtypeStruct(shape, jnp.float32),
-        in_specs=[pl.BlockSpec(memory_space=pltpu.VMEM)],
-        out_specs=pl.BlockSpec(memory_space=pltpu.VMEM),
-        scratch_shapes=[
-            pltpu.VMEM((3,) + shape, jnp.float32),
-            pltpu.SemaphoreType.DMA((3,)),
-            pltpu.SemaphoreType.DMA((3,)),
-        ],
-        compiler_params=pltpu.CompilerParams(collective_id=2, has_side_effects=True),
-    )(value)[:1, :1]
 
 
 def scaled(rows, sum_squares, bond_left, bond_mid, bond_right, is_left):
@@ -712,23 +863,17 @@
 
 
 def local(sites, start, gates, bonds):
+    if lax.axis_size("bond") == 4:
+        rows, factor = pair_step(gates, bonds, sites[0], start[0])
+        return (rows * factor[:1, :1])[None]
+    return spread_out(sites, start, gates, bonds)
+
+
+def spread_out(sites, start, gates, bonds):
+    bond_index = lax.axis_index("bond")
     chain_index = lax.axis_index("chain")
     is_left = chain_index % 2 == 0
     left_site = jnp.where(is_left, chain_index, chain_index - 1)
-    bond_left = bonds[left_site]
-    bond_mid = bonds[left_site + 1]
-    bond_right = bonds[left_site + 2]
-    bounds = jnp.stack([bond_right, bond_mid, jnp.where(is_left, 0, 1)]).astype(jnp.int32)
-    if lax.axis_size("bond") == 4:
-        thetas, x, gram = pair_step(gates, bonds, sites[0], start[0])
-        inverse = factor_inverse(bounds, gram)
-        rows, squares = final_rows(thetas, x, inverse)
-        return scaled(rows, total_of(squares), bond_left, bond_mid, bond_right, is_left)
-    return spread_out(sites, start, gates, bonds, bounds, is_left, left_site)
-
-
-def spread_out(sites, start, gates, bonds, bounds, is_left, left_site):
-    bond_index = lax.axis_index("bond")
     rank_width = start.shape[2]
     local_rows = sites.shape[1]
     own_site = sites[0]
@@ -736,6 +881,7 @@
     bond_left = bonds[left_site]
     bond_mid = bonds[left_site + 1]
     bond_right = bonds[left_site + 2]
+    bounds = jnp.stack([bond_right, bond_mid, jnp.where(is_left, 0, 1)]).astype(jnp.int32)
     columns = jnp.arange(rank_width)
     row_global = bond_index * local_rows + jnp.arange(local_rows)
     mid_keep = columns < bond_mid

time: 159 us -> 125 us (0.79)
  Pallas kernels: 148 us -> 119 us
  between operations: 2.59 us -> 0.01 us
    pallas_call x4 -> x1, Pallas kernels: 148 us -> 119 us  [pair_step(): pl.pallas_call(pair_kernel, out_shape=(jax.ShapeDtypeStruct((rows, wide),...]
    another operation x1 -> x0, other arithmetic: 1.9 us -> none  [local(): jnp.stack([bond_right, bond_mid, jnp.where(is_left, 0, 1)])]
where the time goes in v3:
time: 125 us; the launch traced here: 124 us
  Pallas kernels  119 us (95%)
  other arithmetic  3.74 us (3%)
    pallas_call x1, Pallas kernels, pair_step(): pl.pallas_call(pair_kernel, out_shape=(jax.ShapeDtypeStruct((rows, wide),...  119 us
    broadcast_in_dim x1, other arithmetic, local(): return (rows * factor[:1, :1])[None]  3.74 us

profile of v3, /device:TPU:0, one launch (start us, length us, event | category | flops | bytes accessed | tf_op | source)
XLA Modules:
  0.0 124.0 jit_solution(9973285248837910762)
XLA Ops:
  0.0 119.1 %shard_map.46 = (f32[256,2048]{1,0:T(8,128)}, f32[8,128]{1,0:T(8,128)}) custom-call(f32[8,16]{1,0:T(8,128)} %gate_ref.1, s32[9]{0:T(128)} %bond_ref.1, bf16[256,2048]{1,0:T(8,128)(2,1)} %bitcast.5, bf16[256,1024]{1,0:T(8,128)(2,1)} %bitcast.6), custom_call_target="tpu_custom_call" | custom-call | tf_op jit(solution)/shard_map/pallas_call | solution.py:810
  119.1 1.2 slice.3
  120.3 3.7 %multiply_bitcast_fusion = f32[1,256,2048]{2,1,0:T(8,128)} fusion(f32[256,2048]{1,0:T(8,128)} %get-tuple-element.7, f32[]{:T(128)} %bitcast.2), kind=kLoop, calls=%fused_computation | loop fusion | flops 524288 | bytes 4194308 | tf_op jit(solution)/shard_map/broadcast_in_dim | solution.py:868

commit v4 on v3

--- a/solution.py
+++ b/solution.py
@@ -738,20 +738,18 @@
                     - jnp.dot(threewide(side.T), threefold(side), preferred_element_type=jnp.float32)
                 )
                 if c + 1 < chunks:
-                    pass_on(c + 1)
                     to_mate(c + 1)
-                    if c + 2 < chunks:
-                        offer(c + 2)
-
-            if c + 1 < chunks:
-
-                @pl.when(p == 1)
-                def _():
                     last_to_mate(c + 1)
 
             return carry
 
+        if c + 1 < chunks:
+            pass_on(c + 1)
+        if c + 2 < chunks:
+            offer(c + 2)
         lax.fori_loop(0, CHUNK // BLOCK, panel, 0)
+        if c + 1 < chunks:
+            arrive(c + 1)
         corner = -jnp.dot(threewide(inverses[1]), threefold(below[...]), preferred_element_type=jnp.float32)
         own_inverse = jnp.concatenate(
             [
@@ -772,9 +770,6 @@
             whole[0, here, :start] = top
             whole[1, here, :start] = low_part
 
-        if c + 1 < chunks:
-            arrive(c + 1)
-
     @pl.when(core == 0)
     def _():
         for o in range(2):
@@ -797,7 +792,7 @@
 
     mean_square = total / (2.0 * real(kept_left) * real(kept_mid)) + 1e-06
     factor = jnp.where(core == 0, lax.rsqrt(mean_square), jnp.sqrt(2.0 * real(kept_right)))
-    factor_ref[...] = jnp.broadcast_to(factor, (SUB, BLOCK))
+    factor_ref[...] = factor
     links.drain()
 
 
@@ -811,7 +806,7 @@
         pair_kernel,
         out_shape=(
             jax.ShapeDtypeStruct((rows, wide), jnp.float32),
-            jax.ShapeDtypeStruct((SUB, BLOCK), jnp.float32),
+            jax.ShapeDtypeStruct((1, 1), jnp.float32),
         ),
         in_specs=[pl.BlockSpec(memory_space=pltpu.SMEM)] * 2 + [pl.BlockSpec(memory_space=pltpu.HBM)] * 2,
         out_specs=(pl.BlockSpec(memory_space=pltpu.VMEM),) * 2,
@@ -865,7 +860,7 @@
 def local(sites, start, gates, bonds):
     if lax.axis_size("bond") == 4:
         rows, factor = pair_step(gates, bonds, sites[0], start[0])
-        return (rows * factor[:1, :1])[None]
+        return (rows * factor)[None]
     return spread_out(sites, start, gates, bonds)
 
 

time: 125 us -> 119 us (0.952)
  Pallas kernels: 119 us -> 114 us
    pallas_call x1, Pallas kernels: 119 us -> 114 us  [pair_step(): pl.pallas_call(pair_kernel, out_shape=(jax.ShapeDtypeStruct((rows, wide),...]
where the time goes in v4:
time: 119 us; the launch traced here: 118 us
  Pallas kernels  114 us (96%)
  other arithmetic  3.73 us (3%)
    pallas_call x1, Pallas kernels, pair_step(): pl.pallas_call(pair_kernel, out_shape=(jax.ShapeDtypeStruct((rows, wide),...  114 us
    broadcast_in_dim x1, other arithmetic, local(): return (rows * factor)[None]  3.73 us

profile of v4, /device:TPU:0, one launch (start us, length us, event | category | flops | bytes accessed | tf_op | source)
XLA Modules:
  0.0 117.8 jit_solution(4218082052448020682)
XLA Ops:
  0.0 114.0 %shard_map.46 = (f32[256,2048]{1,0:T(8,128)}, f32[1,1]{1,0:T(1,128)}) custom-call(f32[8,16]{1,0:T(8,128)} %gate_ref.1, s32[9]{0:T(128)} %bond_ref.1, bf16[256,2048]{1,0:T(8,128)(2,1)} %bitcast.5, bf16[256,1024]{1,0:T(8,128)(2,1)} %bitcast.6), custom_call_target="tpu_custom_call" | custom-call | tf_op jit(solution)/shard_map/pallas_call | solution.py:805
  114.0 3.7 %multiply_bitcast_fusion = f32[1,256,2048]{2,1,0:T(8,128)} fusion(f32[256,2048]{1,0:T(8,128)} %get-tuple-element.7, f32[]{:T(128)} %bitcast.2), kind=kLoop, calls=%fused_computation | loop fusion | flops 524288 | bytes 4194308 | tf_op jit(solution)/shard_map/broadcast_in_dim | solution.py:863

commit v5 on v4

--- a/solution.py
+++ b/solution.py
@@ -842,7 +842,7 @@
             pltpu.SemaphoreType.DMA((3,)),
         ],
         compiler_params=pltpu.CompilerParams(
-            collective_id=0, has_side_effects=True, vmem_limit_bytes=57 * 1024 * 1024
+            collective_id=0, has_side_effects=True, vmem_limit_bytes=49 * 1024 * 1024
         ),
     )(gates, bonds, own_site, own_start)
 
@@ -859,7 +859,8 @@
 
 def local(sites, start, gates, bonds):
     if lax.axis_size("bond") == 4:
-        rows, factor = pair_step(gates, bonds, sites[0], start[0])
+        held = [pltpu.with_memory_space_constraint(x, pltpu.HBM) for x in (gates, bonds, sites[0], start[0])]
+        rows, factor = pair_step(*held)
         return (rows * factor)[None]
     return spread_out(sites, start, gates, bonds)
 

time: 119 us -> 117 us (0.983)
  other arithmetic: 3.73 us -> 2.09 us
    broadcast_in_dim x1, other arithmetic: 3.73 us -> 2.09 us  [local(): return (rows * factor)[None]]
where the time goes in v5:
time: 117 us; the launch traced here: 115 us
  Pallas kernels  113 us (97%)
  other arithmetic  2.09 us (2%)
    pallas_call x1, Pallas kernels, pair_step(): pl.pallas_call(pair_kernel, out_shape=(jax.ShapeDtypeStruct((rows, wide),...  113 us

profile of v5, /device:TPU:0, one launch (start us, length us, event | category | flops | bytes accessed | tf_op | source)
XLA Modules:
  0.0 115.3 jit_solution(11918373246435783765)
XLA Ops:
  0.0 113.2 %shard_map.46 = (f32[256,2048]{1,0:T(8,128)S(1)}, f32[1,1]{1,0:T(1,128)}) custom-call(f32[8,16]{1,0:T(8,128)} %gate_ref.1, s32[9]{0:T(128)} %bond_ref.1, bf16[256,2048]{1,0:T(8,128)(2,1)} %bitcast.5, bf16[256,1024]{1,0:T(8,128)(2,1)} %bitcast.6), custom_call_target="tpu_custom_call" | custom-call | tf_op jit(solution)/shard_map/pallas_call | solution.py:805
  113.2 2.1 %multiply_bitcast_fusion = f32[1,256,2048]{2,1,0:T(8,128)} fusion(f32[256,2048]{1,0:T(8,128)S(1)} %get-tuple-element.7, f32[]{:T(128)} %bitcast.2), kind=kLoop, calls=%fused_computation | loop fusion | flops 524288 | bytes 4194308 | tf_op jit(solution)/shard_map/broadcast_in_dim | solution.py:864
